TPU v7x, 32 devices: a whole 2x2x4 slice. The times are simulated.
32 devices in a mesh: dp: 4 (over y, x), tensor: 8 (over z, core).
Axes of the slice: x: 2, y: 2, z: 4, core: 2. Of those that a mesh axis runs over, the one named last changes fastest.
Arguments:
- hidden_x: bfloat16 [32, 128, 16384], P('dp', None, 'tensor'), may hold values from -6 to 6
- gate_z: bfloat16 [32, 128, 16384], P('dp', None, 'tensor'), may hold values from -6 to 6
- conv_weight: float32 [4, 16384], P(None, 'tensor'), may hold values from -3 to 3
- conv_bias: float32 [16384], P('tensor'), may hold values from -0.5 to 0.5
- x_weight: bfloat16 [16384, 544], P('tensor'), may hold values from -0.046875 to 0.046875
- dt_weight: bfloat16 [512, 16384], P(None, 'tensor'), may hold values from -0.25 to 0.25
- dt_bias: float32 [16384], P('tensor'), may hold values from -6 to -2
- a_log: float32 [16, 16384], P(None, 'tensor'), may hold values from -2 to 2.7
- skip_gain: float32 [16384], P('tensor'), may hold values from 0.5 to 1.5
- ssm_cache: float32 [32, 16, 16384], P('dp', None, 'tensor'), may hold values from -6 to 6
- conv_cache: float32 [32, 3, 16384], P('dp', None, 'tensor'), may hold values from -6 to 6
- holder_of: int32 [32], replicated, may hold values from 0 to 3, as said below
- slot_of: int32 [32], replicated, may hold values from 0 to 7, as said below
Outputs:
- gated_out: bfloat16 [32, 128, 16384], P('dp', None, 'tensor')
- new_ssm: float32 [32, 16, 16384], P('dp', None, 'tensor')
- new_conv: float32 [32, 3, 16384], P('dp', None, 'tensor')
Inputs may be any that keep to these rules, and one draw needn't show every extreme that they name: `holder_of`: requests 8 * g to 8 * g + 7 belong to dp group g. One holder serves at most 2 requests of one group, and in every group some holder serves exactly 2. `slot_of`: requests with the same holder have different slots.
All inputs are finite; a program needn't handle non-finite values.
Results may differ from a plain program's by a relative error of at most 0.0062.
Values may be sent and summed in bfloat16 or wider, within the bound.
A program may use at most 128 MiB of HBM per device.

v0:
```python
import jax
import jax.numpy as jnp
from jax import lax
from jax.sharding import PartitionSpec as P

EPSILON = 1e-06
NORM_FLOOR = 0.25


def normalize(projected, rank_width, state_width):
    dt_raw = projected[:, :rank_width]
    inject_raw = projected[:, rank_width : rank_width + state_width]
    readout_raw = projected[:, rank_width + state_width :]
    dt_norm = dt_raw * lax.rsqrt(jnp.mean(dt_raw * dt_raw, axis=1, keepdims=True) + EPSILON)
    inject_norm = inject_raw * lax.rsqrt(
        jnp.maximum(jnp.mean(inject_raw * inject_raw, axis=1, keepdims=True), NORM_FLOOR)
    )
    readout_norm = readout_raw * lax.rsqrt(
        jnp.maximum(jnp.mean(readout_raw * readout_raw, axis=1, keepdims=True), NORM_FLOOR)
    )
    joined = jnp.concatenate([inject_norm, readout_norm], axis=1)
    return (dt_norm.astype(jnp.bfloat16), joined.astype(jnp.bfloat16))


def convolve(hidden_rows, conv_start, conv_weight, conv_bias):
    turn_len = hidden_rows.shape[1]
    extended = jnp.concatenate([conv_start, hidden_rows.astype(jnp.float32)], axis=1)
    summed = jnp.zeros(hidden_rows.shape, jnp.float32) + conv_bias[None, None, :]
    for offset in range(conv_weight.shape[0]):
        summed = (
            summed + extended[:, offset : offset + turn_len, :] * conv_weight[offset][None, None, :]
        )
    return jax.nn.silu(summed).astype(jnp.bfloat16)


def advance(carried, decay_rate, dt_now, drive_now, inject_now, readout_now):
    carried = (
        jnp.exp(dt_now[:, None, :] * decay_rate[None, :, :]) * carried
        + drive_now[:, None, :] * inject_now[:, :, None]
    )
    return (carried, jnp.sum(readout_now[:, :, None] * carried, axis=1))


def recur_blocks(
    state_start, decay_rate, dt_full, drive_full, inject_full, readout_full, block_len
):

    def time_major(values):
        moved = jnp.swapaxes(values, 0, 1)
        return moved.reshape((moved.shape[0] // block_len, block_len) + moved.shape[1:])

    def one_block(carried, slices):
        dt_block, drive_block, inject_block, readout_block = slices
        outputs = []
        for offset in range(block_len):
            carried, output_now = advance(
                carried,
                decay_rate,
                dt_block[offset],
                drive_block[offset],
                inject_block[offset],
                readout_block[offset],
            )
            outputs.append(output_now)
        return (carried, jnp.stack(outputs))

    final_state, readout = lax.scan(
        one_block,
        state_start,
        (
            time_major(dt_full),
            time_major(drive_full),
            time_major(inject_full),
            time_major(readout_full),
        ),
    )
    readout = readout.reshape((-1,) + readout.shape[2:])
    return (final_state, jnp.swapaxes(readout, 0, 1))


def body(
    hidden_x,
    gate_z,
    conv_weight,
    conv_bias,
    x_weight,
    dt_weight,
    dt_bias,
    a_log,
    skip_gain,
    ssm_cache,
    conv_cache,
    holder_of,
    slot_of,
):
    groups = lax.axis_size("dp")
    my_index = lax.axis_index("dp")
    requests = hidden_x.shape[0]
    slot_count = ssm_cache.shape[0]
    capacity = slot_count // groups
    state_width = a_log.shape[0]
    rank_width = dt_weight.shape[0]
    holders = holder_of.reshape(groups, requests)
    places = slot_of.reshape(groups, requests)
    earlier = jnp.arange(requests)[None, :] < jnp.arange(requests)[:, None]
    same_holder = holders[:, :, None] == holders[:, None, :]
    rank_within = jnp.sum((same_holder & earlier[None, :, :]).astype(jnp.int32), axis=2)
    rank_range = jnp.arange(capacity, dtype=jnp.int32)
    served = (holders == my_index)[:, None, :] & (
        rank_within[:, None, :] == rank_range[None, :, None]
    )
    occupied = jnp.any(served, axis=2)
    sources = jnp.sum(jnp.where(served, places[:, None, :], 0), axis=2)
    outgoing = (ssm_cache[sources], conv_cache[sources])
    arrived = (
        lax.all_to_all(outgoing[0], "dp", split_axis=0, concat_axis=0, tiled=True),
        lax.all_to_all(outgoing[1], "dp", split_axis=0, concat_axis=0, tiled=True),
    )
    own_holders = holders[my_index]
    own_ranks = rank_within[my_index]
    lookup = own_holders * capacity + own_ranks
    state_start = arrived[0].reshape((groups * capacity,) + arrived[0].shape[2:])[lookup]
    conv_start = arrived[1].reshape((groups * capacity,) + arrived[1].shape[2:])[lookup]
    conv_out = convolve(hidden_x, conv_start, conv_weight, conv_bias)
    flat_rows = conv_out.reshape(-1, conv_out.shape[2])
    row_share = lax.psum_scatter(
        jnp.dot(flat_rows, x_weight, preferred_element_type=jnp.float32),
        "tensor",
        scatter_dimension=0,
        tiled=True,
    )
    dt_share, bc_share = normalize(row_share, rank_width, state_width)
    dt_norm, bc_norm = (
        lax.all_gather(dt_share, "tensor", axis=0, tiled=True),
        lax.all_gather(bc_share, "tensor", axis=0, tiled=True),
    )
    dt_full = jax.nn.softplus(
        jnp.dot(dt_norm, dt_weight, preferred_element_type=jnp.float32) + dt_bias[None, :]
    )
    dt_full = dt_full.reshape(hidden_x.shape)
    drive_full = dt_full * conv_out.astype(jnp.float32)
    bc_full = bc_norm.astype(jnp.float32).reshape(
        hidden_x.shape[0], hidden_x.shape[1], 2 * state_width
    )
    decay_rate = -jnp.exp(a_log)
    final_state, readout = recur_blocks(
        state_start,
        decay_rate,
        dt_full,
        drive_full,
        bc_full[:, :, :state_width],
        bc_full[:, :, state_width:],
        8,
    )
    gated_out = (
        (readout + skip_gain[None, None, :] * conv_out.astype(jnp.float32))
        * jax.nn.silu(gate_z.astype(jnp.float32))
    ).astype(jnp.bfloat16)
    kept_rows = conv_cache.shape[1]
    last_inputs = hidden_x[:, hidden_x.shape[1] - kept_rows :, :].astype(jnp.float32)
    placed = (own_holders[None, None, :] == jnp.arange(groups, dtype=jnp.int32)[:, None, None]) & (
        own_ranks[None, None, :] == rank_range[None, :, None]
    )
    picked_rows = jnp.sum(
        jnp.where(placed, jnp.arange(requests, dtype=jnp.int32)[None, None, :], 0), axis=2
    )
    received = (
        lax.all_to_all(
            final_state[picked_rows].astype(jnp.bfloat16),
            "dp",
            split_axis=0,
            concat_axis=0,
            tiled=True,
        ).astype(jnp.float32),
        lax.all_to_all(
            last_inputs[picked_rows].astype(jnp.bfloat16),
            "dp",
            split_axis=0,
            concat_axis=0,
            tiled=True,
        ).astype(jnp.float32),
    )
    targets = jnp.where(occupied, sources, slot_count).reshape(-1)
    new_ssm = ssm_cache.at[targets].set(
        received[0].reshape((-1,) + received[0].shape[2:]), mode="drop"
    )
    new_conv = conv_cache.at[targets].set(
        received[1].reshape((-1,) + received[1].shape[2:]), mode="drop"
    )
    return (gated_out, new_ssm, new_conv)


def solution(mesh):
    placed = (
        P("dp", None, "tensor"),
        P("dp", None, "tensor"),
        P(None, "tensor"),
        P("tensor"),
        P("tensor", None),
        P(None, "tensor"),
        P("tensor"),
        P(None, "tensor"),
        P("tensor"),
        P("dp", None, "tensor"),
        P("dp", None, "tensor"),
        P(),
        P(),
    )
    return jax.shard_map(
        body,
        mesh=mesh,
        in_specs=placed,
        out_specs=(P("dp", None, "tensor"), P("dp", None, "tensor"), P("dp", None, "tensor")),
        check_vma=False,
    )
```

profile of v0, /device:TPU:0, one launch (start us, length us, event | category | flops | bytes accessed | tf_op | source)
XLA Modules:
  0.0 384.1 jit_solution(17809938325671926567)
XLA Ops:
  16.4 5.2 %all-to-all-start.1 = ((f32[4,2,3,2048]{3,1,2,0:T(2,128)}), f32[4,2,3,2048]{3,1,2,0:T(2,128)}, u32[]{:S(2)}, u32[]{:S(2)}) async-start(f32[4,2,3,2048]{3,1,2,0:T(2,128)} %copy.85), calls=%async_computation.1 | async-start | bytes 393216 | tf_op jit(solution)/shard_map/all_to_all | solution.py:117
  22.5 6.5 %convert_element_type.36 = f32[8,128,2048]{2,1,0:T(8,128)} convert(bf16[8,128,2048]{2,1,0:T(8,128)(2,1)} %param.15) | non-fusion elementwise | flops 2097152 | bytes 12582912 | tf_op jit(solution)/shard_map/convert_element_type | solution.py:27
  29.0 1.8 copy.86
  30.8 2.3 gather_fusion.3
  33.1 13.1 %multiply_convert_fusion = bf16[8,128,2048]{2,1,0:T(8,128)(2,1)S(1)} fusion(f32[8,128,2048]{2,1,0:T(8,128)} %convert_element_type.36, f32[8,3,2048]{2,1,0:T(4,128)} %gather_fusion.3, f32[2048]{0:T(1024)S(1)} %bitcast.252, f32[2048]{0:T(1024)S(1)} %bitcast.253, f32[2048]{0:T(1024)S(1)} %bitcast.251, f32[2048]{0:T(1024)S(1)} %bitcast.250, f32[2048]{0:T(1024)S(1)} %copy-done.7), kind=kLoop, calls=%fused_computation.123 | loop fusion | flops 33554432 | bytes 12820480 | tf_op jit(solution)/shard_map/convert_element_type | solution.py:33
  46.3 2.0 copy-done.3
  48.3 3.9 %fusion.39 = f32[1024,544]{0,1:T(8,128)} fusion(bf16[1024,2048]{1,0:T(8,128)(2,1)S(1)} %bitcast.215, bf16[2048,544]{0,1:T(8,128)(2,1)S(1)} %copy-done), kind=kOutput, calls=%fused_computation.167 | convolution fusion | flops 2281701376 | bytes 8650752 | tf_op jit(solution)/shard_map/dot_general | solution.py:127
  55.2 4.2 %all-to-all-start.3 = ((bf16[4,2,3,2048]{3,1,2,0:T(2,128)(2,1)}), bf16[4,2,3,2048]{3,1,2,0:T(2,128)(2,1)S(1)}, u32[]{:S(2)}, u32[]{:S(2)}) async-start(bf16[4,2,3,2048]{3,1,2,0:T(2,128)(2,1)} %copy.95), calls=%async_computation.4 | async-start | bytes 196608 | tf_op jit(solution)/shard_map/all_to_all | solution.py:175
  62.2 28.6 %reduce-scatter.2.cloned.1.call-done = f32[128,544]{0,1:T(8,128)} async-done(((f32[1024,544]{0,1:T(8,128)}), f32[128,544]{0,1:T(8,128)}) %reduce-scatter.2.cloned.1.call-update) | async-done | bytes 278544 | tf_op jit(solution)/shard_map/reduce_scatter | solution.py:126
  91.9 3.8 all-to-all-start
  99.1 7.5 %all-to-all-done = f32[4,2,16,2048]{3,2,1,0:T(8,128)S(1)} async-done(((f32[4,2,16,2048]{3,2,1,0:T(8,128)}), f32[4,2,16,2048]{3,2,1,0:T(8,128)S(1)}, u32[]{:S(2)}, u32[]{:S(2)}) %all-to-all-start) | async-done | bytes 1048608 | tf_op jit(solution)/shard_map/all_to_all | solution.py:116
  108.7 13.2 %all_gather.7 = bf16[1024,32]{0,1:T(8,128)(2,1)S(1)} all-gather(bf16[128,32]{0,1:T(8,128)(2,1)S(1)} %pad_maximum_fusion.1), channel_id=1, replica_groups=mesh['dp'=4,'tensor'=8] {'tensor'}, dimensions={0}, use_global_device_ids=true | all-gather | bytes 73728 | tf_op jit(solution)/shard_map/all_gather | solution.py:135
  124.1 11.5 %compare_select_fusion = f32[1024,2048]{1,0:T(8,128)} fusion(f32[2048]{0:T(1024)S(1)} %copy-done.8, bf16[1024,512]{0,1:T(8,128)(2,1)} %all-gather.2.cloned.1.call-done, bf16[512,2048]{1,0:T(8,128)(2,1)} %param.20), kind=kOutput, calls=%fused_computation.97 | convolution fusion | flops 2162163712 | bytes 11542528 | tf_op jit(solution)/shard_map/dot_general | solution.py:138
  135.6 8.7 %fusion.24 = f32[16,8,8,2048]{3,1,0,2:T(8,128)} fusion(f32[8,128,2048]{2,1,0:T(8,128)} %bitcast.241, bf16[8,128,2048]{2,1,0:T(8,128)(2,1)S(1)} %copy-done.4), kind=kLoop, calls=%fused_computation.114 | loop fusion | flops 4194304 | bytes 20971520 | tf_op jit(solution)/shard_map/reshape | solution.py:50
  144.3 213.5 %while.12 = (s32[]{:T(128)}, f32[8,16,2048]{2,1,0:T(8,128)S(1)}, f32[16,8,8,2048]{3,1,0,2:T(8,128)}, f32[16,8,8,2048]{3,1,0,2:T(8,128)}, f32[16,2048]{1,0:T(8,12...) while((s32[]{:T(128)}, f32[8,16,2048]{2,1,0:T(8,128)S(1)}, ...), condition=%wide.region_15.16_spmd, body=%wide.region_6.15_spmd.sunk | while | flops 18743304 | bytes 14314813 | solution.py:67
  145.1 5.0 %constant_dynamic-slice_fusion.35 = (f32[1,1,8,2048]{3,1,0,2:T(1,128)S(1)}, f32[1,1,8,2048]{3,1,0,2:T(1,128)S(1)}, f32[1,1,8,2048]{3,1,0,2:T(1,128)S(1)}, f32[1,...) fusion(f32[16,8,8,2048]{3,1,0,2:T(8,128)} %get-tuple-element.36, ...), kind=kLoop, calls=%fused_computation.69.clone.1 | loop fusion | bytes 2097184 | tf_op jit(solution)/shard_map/while/body/eval_jaxpr/slice | solution.py:60
  152.1 2.5 multiply_reduce_fusion.14
  154.6 1.7 multiply_reduce_fusion.16
  158.3 5.4 %constant_dynamic-slice_fusion.35 = (f32[1,1,8,2048]{3,1,0,2:T(1,128)S(1)}, f32[1,1,8,2048]{3,1,0,2:T(1,128)S(1)}, f32[1,1,8,2048]{3,1,0,2:T(1,128)S(1)}, f32[1,...) fusion(f32[16,8,8,2048]{3,1,0,2:T(8,128)} %get-tuple-element.36, ...), kind=kLoop, calls=%fused_computation.69.clone.1 | loop fusion | bytes 2097184 | tf_op jit(solution)/shard_map/while/body/eval_jaxpr/slice | solution.py:60
  165.7 2.5 multiply_reduce_fusion.14
  168.2 1.7 multiply_reduce_fusion.16
  171.9 5.3 %constant_dynamic-slice_fusion.35 = (f32[1,1,8,2048]{3,1,0,2:T(1,128)S(1)}, f32[1,1,8,2048]{3,1,0,2:T(1,128)S(1)}, f32[1,1,8,2048]{3,1,0,2:T(1,128)S(1)}, f32[1,...) fusion(f32[16,8,8,2048]{3,1,0,2:T(8,128)} %get-tuple-element.36, ...), kind=kLoop, calls=%fused_computation.69.clone.1 | loop fusion | bytes 2097184 | tf_op jit(solution)/shard_map/while/body/eval_jaxpr/slice | solution.py:60
  179.2 2.5 multiply_reduce_fusion.14
  181.7 1.7 multiply_reduce_fusion.16
  185.5 5.1 %constant_dynamic-slice_fusion.35 = (f32[1,1,8,2048]{3,1,0,2:T(1,128)S(1)}, f32[1,1,8,2048]{3,1,0,2:T(1,128)S(1)}, f32[1,1,8,2048]{3,1,0,2:T(1,128)S(1)}, f32[1,...) fusion(f32[16,8,8,2048]{3,1,0,2:T(8,128)} %get-tuple-element.36, ...), kind=kLoop, calls=%fused_computation.69.clone.1 | loop fusion | bytes 2097184 | tf_op jit(solution)/shard_map/while/body/eval_jaxpr/slice | solution.py:60
  192.5 2.5 multiply_reduce_fusion.14
  195.0 1.7 multiply_reduce_fusion.16
  198.8 5.0 %constant_dynamic-slice_fusion.35 = (f32[1,1,8,2048]{3,1,0,2:T(1,128)S(1)}, f32[1,1,8,2048]{3,1,0,2:T(1,128)S(1)}, f32[1,1,8,2048]{3,1,0,2:T(1,128)S(1)}, f32[1,...) fusion(f32[16,8,8,2048]{3,1,0,2:T(8,128)} %get-tuple-element.36, ...), kind=kLoop, calls=%fused_computation.69.clone.1 | loop fusion | bytes 2097184 | tf_op jit(solution)/shard_map/while/body/eval_jaxpr/slice | solution.py:60
  205.8 2.5 multiply_reduce_fusion.14
  208.3 1.7 multiply_reduce_fusion.16
  212.0 5.6 %constant_dynamic-slice_fusion.35 = (f32[1,1,8,2048]{3,1,0,2:T(1,128)S(1)}, f32[1,1,8,2048]{3,1,0,2:T(1,128)S(1)}, f32[1,1,8,2048]{3,1,0,2:T(1,128)S(1)}, f32[1,...) fusion(f32[16,8,8,2048]{3,1,0,2:T(8,128)} %get-tuple-element.36, ...), kind=kLoop, calls=%fused_computation.69.clone.1 | loop fusion | bytes 2097184 | tf_op jit(solution)/shard_map/while/body/eval_jaxpr/slice | solution.py:60
  219.6 2.5 multiply_reduce_fusion.14
  222.1 1.7 multiply_reduce_fusion.16
  225.8 5.2 %constant_dynamic-slice_fusion.35 = (f32[1,1,8,2048]{3,1,0,2:T(1,128)S(1)}, f32[1,1,8,2048]{3,1,0,2:T(1,128)S(1)}, f32[1,1,8,2048]{3,1,0,2:T(1,128)S(1)}, f32[1,...) fusion(f32[16,8,8,2048]{3,1,0,2:T(8,128)} %get-tuple-element.36, ...), kind=kLoop, calls=%fused_computation.69.clone.1 | loop fusion | bytes 2097184 | tf_op jit(solution)/shard_map/while/body/eval_jaxpr/slice | solution.py:60
  233.0 2.5 multiply_reduce_fusion.14
  235.5 1.7 multiply_reduce_fusion.16
  239.3 5.1 %constant_dynamic-slice_fusion.35 = (f32[1,1,8,2048]{3,1,0,2:T(1,128)S(1)}, f32[1,1,8,2048]{3,1,0,2:T(1,128)S(1)}, f32[1,1,8,2048]{3,1,0,2:T(1,128)S(1)}, f32[1,...) fusion(f32[16,8,8,2048]{3,1,0,2:T(8,128)} %get-tuple-element.36, ...), kind=kLoop, calls=%fused_computation.69.clone.1 | loop fusion | bytes 2097184 | tf_op jit(solution)/shard_map/while/body/eval_jaxpr/slice | solution.py:60
  246.4 2.5 multiply_reduce_fusion.14
  248.9 1.7 multiply_reduce_fusion.16
  252.6 5.1 %constant_dynamic-slice_fusion.35 = (f32[1,1,8,2048]{3,1,0,2:T(1,128)S(1)}, f32[1,1,8,2048]{3,1,0,2:T(1,128)S(1)}, f32[1,1,8,2048]{3,1,0,2:T(1,128)S(1)}, f32[1,...) fusion(f32[16,8,8,2048]{3,1,0,2:T(8,128)} %get-tuple-element.36, ...), kind=kLoop, calls=%fused_computation.69.clone.1 | loop fusion | bytes 2097184 | tf_op jit(solution)/shard_map/while/body/eval_jaxpr/slice | solution.py:60
  259.7 2.5 multiply_reduce_fusion.14
  262.2 1.7 multiply_reduce_fusion.16
  265.9 5.0 %constant_dynamic-slice_fusion.35 = (f32[1,1,8,2048]{3,1,0,2:T(1,128)S(1)}, f32[1,1,8,2048]{3,1,0,2:T(1,128)S(1)}, f32[1,1,8,2048]{3,1,0,2:T(1,128)S(1)}, f32[1,...) fusion(f32[16,8,8,2048]{3,1,0,2:T(8,128)} %get-tuple-element.36, ...), kind=kLoop, calls=%fused_computation.69.clone.1 | loop fusion | bytes 2097184 | tf_op jit(solution)/shard_map/while/body/eval_jaxpr/slice | solution.py:60
  273.0 2.5 multiply_reduce_fusion.14
  275.4 1.7 multiply_reduce_fusion.16
  279.2 5.0 %constant_dynamic-slice_fusion.35 = (f32[1,1,8,2048]{3,1,0,2:T(1,128)S(1)}, f32[1,1,8,2048]{3,1,0,2:T(1,128)S(1)}, f32[1,1,8,2048]{3,1,0,2:T(1,128)S(1)}, f32[1,...) fusion(f32[16,8,8,2048]{3,1,0,2:T(8,128)} %get-tuple-element.36, ...), kind=kLoop, calls=%fused_computation.69.clone.1 | loop fusion | bytes 2097184 | tf_op jit(solution)/shard_map/while/body/eval_jaxpr/slice | solution.py:60
  286.1 2.5 multiply_reduce_fusion.14
  288.6 1.7 multiply_reduce_fusion.16
  292.3 5.2 %constant_dynamic-slice_fusion.35 = (f32[1,1,8,2048]{3,1,0,2:T(1,128)S(1)}, f32[1,1,8,2048]{3,1,0,2:T(1,128)S(1)}, f32[1,1,8,2048]{3,1,0,2:T(1,128)S(1)}, f32[1,...) fusion(f32[16,8,8,2048]{3,1,0,2:T(8,128)} %get-tuple-element.36, ...), kind=kLoop, calls=%fused_computation.69.clone.1 | loop fusion | bytes 2097184 | tf_op jit(solution)/shard_map/while/body/eval_jaxpr/slice | solution.py:60
  299.6 2.5 multiply_reduce_fusion.14
  302.0 1.7 multiply_reduce_fusion.16
  305.8 4.9 %constant_dynamic-slice_fusion.35 = (f32[1,1,8,2048]{3,1,0,2:T(1,128)S(1)}, f32[1,1,8,2048]{3,1,0,2:T(1,128)S(1)}, f32[1,1,8,2048]{3,1,0,2:T(1,128)S(1)}, f32[1,...) fusion(f32[16,8,8,2048]{3,1,0,2:T(8,128)} %get-tuple-element.36, ...), kind=kLoop, calls=%fused_computation.69.clone.1 | loop fusion | bytes 2097184 | tf_op jit(solution)/shard_map/while/body/eval_jaxpr/slice | solution.py:60
  312.7 2.5 multiply_reduce_fusion.14
  315.1 1.7 multiply_reduce_fusion.16
  318.9 5.0 %constant_dynamic-slice_fusion.35 = (f32[1,1,8,2048]{3,1,0,2:T(1,128)S(1)}, f32[1,1,8,2048]{3,1,0,2:T(1,128)S(1)}, f32[1,1,8,2048]{3,1,0,2:T(1,128)S(1)}, f32[1,...) fusion(f32[16,8,8,2048]{3,1,0,2:T(8,128)} %get-tuple-element.36, ...), kind=kLoop, calls=%fused_computation.69.clone.1 | loop fusion | bytes 2097184 | tf_op jit(solution)/shard_map/while/body/eval_jaxpr/slice | solution.py:60
  325.9 2.5 multiply_reduce_fusion.14
  332.2 5.0 %constant_dynamic-slice_fusion.35 = (f32[1,1,8,2048]{3,1,0,2:T(1,128)S(1)}, f32[1,1,8,2048]{3,1,0,2:T(1,128)S(1)}, f32[1,1,8,2048]{3,1,0,2:T(1,128)S(1)}, f32[1,...) fusion(f32[16,8,8,2048]{3,1,0,2:T(8,128)} %get-tuple-element.36, ...), kind=kLoop, calls=%fused_computation.69.clone.1 | loop fusion | bytes 2097184 | tf_op jit(solution)/shard_map/while/body/eval_jaxpr/slice | solution.py:60
  339.2 2.5 multiply_reduce_fusion.14
  345.5 4.8 %constant_dynamic-slice_fusion.35 = (f32[1,1,8,2048]{3,1,0,2:T(1,128)S(1)}, f32[1,1,8,2048]{3,1,0,2:T(1,128)S(1)}, f32[1,1,8,2048]{3,1,0,2:T(1,128)S(1)}, f32[1,...) fusion(f32[16,8,8,2048]{3,1,0,2:T(8,128)} %get-tuple-element.36, ...), kind=kLoop, calls=%fused_computation.69.clone.1 | loop fusion | bytes 2097184 | tf_op jit(solution)/shard_map/while/body/eval_jaxpr/slice | solution.py:60
  352.3 2.5 multiply_reduce_fusion.14
  359.1 4.1 %all-to-all-start.2 = ((bf16[4,2,16,2048]{3,2,1,0:T(8,128)(2,1)}), bf16[4,2,16,2048]{3,2,1,0:T(8,128)(2,1)}, u32[]{:S(2)}, u32[]{:S(2)}) async-start(bf16[4,2,16,2048]{3,2,1,0:T(8,128)(2,1)} %bitcast.67), calls=%async_computation.3 | async-start | bytes 1048576 | tf_op jit(solution)/shard_map/all_to_all | solution.py:168
  363.3 8.9 %fusion.27 = bf16[8,128,2048]{2,1,0:T(8,128)(2,1)} fusion(bf16[8,128,2048]{2,1,0:T(8,128)(2,1)} %copy-done.3, bf16[8,128,2048]{2,1,0:T(8,128)(2,1)} %param.16, f32[16,8,8,2048]{3,1,0,2:T(8,128)} %get-tuple-element.46, f32[2048]{0:T(1024)S(1)} %copy-done.6), kind=kLoop, calls=%fused_computation.117 | loop fusion | flops 20971520 | bytes 20979712 | tf_op jit(solution)/shard_map/convert_element_type | solution.py:158
  372.2 2.1 bitcast_convert_fusion
  374.3 2.0 scatter_fusion
  (517 shorter events, 93.3 us)
Async XLA Ops:
  7.2 41.1 %copy-start = (bf16[2048,544]{0,1:T(8,128)(2,1)S(1)}, bf16[2048,544]{0,1:T(8,128)(2,1)}, u32[]{:S(2)}) copy-start(bf16[2048,544]{0,1:T(8,128)(2,1)} %param.19) | copy-start | bytes 6684676
  11.5 21.6 %copy-start.7 = (f32[2048]{0:T(1024)S(1)}, f32[2048]{0:T(1024)}, u32[]{:S(2)}) copy-start(f32[2048]{0:T(1024)} %param.18) | copy-start | bytes 24580
  16.4 12.6 %all-to-all-start.1 = ((f32[4,2,3,2048]{3,1,2,0:T(2,128)}), f32[4,2,3,2048]{3,1,2,0:T(2,128)}, u32[]{:S(2)}, u32[]{:S(2)}) async-start(f32[4,2,3,2048]{3,1,2,0:T(2,128)} %copy.85), calls=%async_computation.1 | async-start | bytes 393216 | tf_op jit(solution)/shard_map/all_to_all | solution.py:117
  21.6 69.3 %reduce-scatter.2.cloned.1.call-start = ((), (), s32[]{:S(2)}) async-start(), calls=%async_computation.5 | async-start | bytes 2506752 | tf_op jit(solution)/shard_map/reduce_scatter | solution.py:126
  46.3 2.0 copy-start.3
  52.2 71.8 %copy-start.8 = (f32[2048]{0:T(1024)S(1)}, f32[2048]{0:T(1024)}, u32[]{:S(2)}) copy-start(f32[2048]{0:T(1024)} %param.21) | copy-start | bytes 24580
  55.2 36.7 %all-to-all-start.3 = ((bf16[4,2,3,2048]{3,1,2,0:T(2,128)(2,1)}), bf16[4,2,3,2048]{3,1,2,0:T(2,128)(2,1)S(1)}, u32[]{:S(2)}, u32[]{:S(2)}) async-start(bf16[4,2,3,2048]{3,1,2,0:T(2,128)(2,1)} %copy.95), calls=%async_computation.4 | async-start | bytes 196608 | tf_op jit(solution)/shard_map/all_to_all | solution.py:175
  91.9 14.7 %all-to-all-start = ((f32[4,2,16,2048]{3,2,1,0:T(8,128)}), f32[4,2,16,2048]{3,2,1,0:T(8,128)S(1)}, u32[]{:S(2)}, u32[]{:S(2)}) async-start(f32[4,2,16,2048]{3,2,1,0:T(8,128)} %bitcast.42), calls=%async_computation | async-start | bytes 2097152 | tf_op jit(solution)/shard_map/all_to_all | solution.py:116
  95.7 28.3 %all-gather.2.cloned.1.call-start = ((), (), s32[]{:S(2)}) async-start(), calls=%async_computation.6 | async-start | bytes 1179648 | tf_op jit(solution)/shard_map/all_gather | solution.py:134
  99.1 36.5 %copy-start.2 = (f32[8,3,2048]{2,0,1:T(8,128)}, f32[8,3,2048]{2,0,1:T(8,128)S(1)}, u32[]{:S(2)}) copy-start(f32[8,3,2048]{2,0,1:T(8,128)S(1)} %scatter_fusion.1) | copy-start | bytes 589828
  124.1 11.5 %copy-start.4 = (bf16[8,128,2048]{2,1,0:T(8,128)(2,1)S(1)}, bf16[8,128,2048]{2,1,0:T(8,128)(2,1)}, u32[]{:S(2)}) copy-start(bf16[8,128,2048]{2,1,0:T(8,128)(2,1)} %copy-done.3) | copy-start | bytes 12582916
  144.3 219.0 %copy-start.6 = (f32[2048]{0:T(1024)S(1)}, f32[2048]{0:T(1024)}, u32[]{:S(2)}) copy-start(f32[2048]{0:T(1024)} %param.23) | copy-start | bytes 24580
  359.1 13.0 %all-to-all-start.2 = ((bf16[4,2,16,2048]{3,2,1,0:T(8,128)(2,1)}), bf16[4,2,16,2048]{3,2,1,0:T(8,128)(2,1)}, u32[]{:S(2)}, u32[]{:S(2)}) async-start(bf16[4,2,16,2048]{3,2,1,0:T(8,128)(2,1)} %bitcast.67), calls=%async_computation.3 | async-start | bytes 1048576 | tf_op jit(solution)/shard_map/all_to_all | solution.py:168
  363.3 14.0 %copy-start.1 = (bf16[2048,544]{0,1:T(8,128)(2,1)S(1)}, bf16[2048,544]{0,1:T(8,128)(2,1)}, u32[]{:S(2)}) copy-start(bf16[2048,544]{0,1:T(8,128)(2,1)} %param.19) | copy-start | bytes 6684676
  376.3 1.0 copy-start.5
Sparse Core Ops, SparseCore 0:
  52.3 38.4 reduce-scatter.1
  98.1 22.9 all-gather.1
where the time goes:
time: 386 us; the launch traced here: 384 us
  local copies, waits for them, and re-layouts  148 us (38%)
  other arithmetic  136 us (35%)
  waiting for transfers between devices  36.2 us (9%)
  starting transfers between devices  17.4 us (5%)
  matrix products  15.4 us (4%)
  between operations  14.3 us (4%)
  blocking collectives  13.2 us (3%)
    reduce_sum x48, other arithmetic, advance(): return (carried, jnp.sum(readout_now[:, :, None] * carried, axis=1))  90.9 us
    slice x16, local copies, waits for them, and re-layouts, one_block(): drive_block[offset]  81.5 us
    reduce_scatter x1, waiting for transfers between devices, body(): lax.psum_scatter(jnp.dot(flat_rows, x_weight, preferred_element_type=jnp....  28.6 us
    dynamic_update_slice x16, local copies, waits for them, and re-layouts, recur_blocks(): lax.scan(one_block, state_start, (time_major(dt_full), time_major(drive_f...  17.5 us
    all_gather x1, blocking collectives, body(): lax.all_gather(bc_share, 'tensor', axis=0, tiled=True)  13.2 us
    convert_element_type x1, other arithmetic, convolve(): return jax.nn.silu(summed).astype(jnp.bfloat16)  13.1 us
    mul x16, local copies, waits for them, and re-layouts, advance(): drive_now[:, None, :] * inject_now[:, :, None]  13 us
    dot_general x1, matrix products, body(): jnp.dot(dt_norm, dt_weight, preferred_element_type=jnp.float32)  11.5 us
  transfers between devices with their start and end apart: 6, of which 2 were waited for; matrix products, arithmetic and copies ran while one was open for 8% of the time, Pallas kernels for 0%

commit v1 on v0

v1 whole, which is shorter than its diff:
```python
import functools

import jax
import jax.numpy as jnp
from jax import lax
from jax.experimental import pallas as pl
from jax.experimental.pallas import tpu as pltpu
from jax.sharding import PartitionSpec as P

EPSILON = 1e-06
NORM_FLOOR = 0.25
LOG2E = 1.4426950408889634
CHUNKS = 2
BLOCK = 256
LANES = 128


def normalize(projected, rank_width, state_width):
    dt_raw = projected[:, :rank_width]
    inject_raw = projected[:, rank_width : rank_width + state_width]
    readout_raw = projected[:, rank_width + state_width :]
    dt_norm = dt_raw * lax.rsqrt(jnp.mean(dt_raw * dt_raw, axis=1, keepdims=True) + EPSILON)
    inject_norm = inject_raw * lax.rsqrt(
        jnp.maximum(jnp.mean(inject_raw * inject_raw, axis=1, keepdims=True), NORM_FLOOR)
    )
    readout_norm = readout_raw * lax.rsqrt(
        jnp.maximum(jnp.mean(readout_raw * readout_raw, axis=1, keepdims=True), NORM_FLOOR)
    )
    return jnp.concatenate([dt_norm, inject_norm, readout_norm], axis=1).astype(jnp.bfloat16)


def conv_kernel(x_ref, start_ref, cw_ref, cb_ref, xw_ref, out_ref, proj_ref, ext):
    step = pl.program_id(0)
    requests, turn, width = x_ref.shape
    taps = cw_ref.shape[0]
    tile = 16
    ext[0 : taps - 1] = start_ref[...]

    def gather(i, _):
        t = pl.multiple_of(i * tile, tile)
        rows = x_ref[:, pl.ds(t, tile), :].astype(jnp.float32)
        ext[pl.ds(taps - 1 + t, tile)] = jnp.swapaxes(rows, 0, 1)
        return 0

    lax.fori_loop(0, turn // tile, gather, 0)
    weights = [cw_ref[j : j + 1, :][None] for j in range(taps)]
    bias = cb_ref[...][None]

    def convolve(i, _):
        t = i * tile
        total = ext[pl.ds(t, tile)] * weights[0] + bias
        for j in range(1, taps):
            total = total + ext[pl.ds(t + j, tile)] * weights[j]
        value = total / (1.0 + jnp.exp(-total))
        row = pl.multiple_of(t * requests, tile * requests)
        out_ref[pl.ds(row, tile * requests), :] = value.reshape(tile * requests, width).astype(
            jnp.bfloat16
        )
        return 0

    lax.fori_loop(0, turn // tile, convolve, 0)

    @pl.when(step == 0)
    def _():
        proj_ref[...] = jnp.dot(out_ref[...], xw_ref[...], preferred_element_type=jnp.float32)

    @pl.when(step > 0)
    def _():
        proj_ref[...] += jnp.dot(out_ref[...], xw_ref[...], preferred_element_type=jnp.float32)


def conv_project(chunk, turn, hidden_x, start, conv_weight, conv_bias, x_weight):
    requests, _, inner = hidden_x.shape
    taps = conv_weight.shape[0]
    cols = x_weight.shape[1]
    rows = requests * turn
    return pl.pallas_call(
        conv_kernel,
        grid=(inner // BLOCK,),
        in_specs=[
            pl.BlockSpec((requests, turn, BLOCK), lambda j: (0, chunk, j)),
            pl.BlockSpec((taps - 1, requests, BLOCK), lambda j: (0, 0, j)),
            pl.BlockSpec((taps, BLOCK), lambda j: (0, j)),
            pl.BlockSpec((1, BLOCK), lambda j: (0, j)),
            pl.BlockSpec((BLOCK, cols), lambda j: (j, 0)),
        ],
        out_specs=[
            pl.BlockSpec((rows, BLOCK), lambda j: (0, j)),
            pl.BlockSpec((rows, cols), lambda j: (0, 0)),
        ],
        out_shape=[
            jax.ShapeDtypeStruct((rows, inner), jnp.bfloat16),
            jax.ShapeDtypeStruct((rows, cols), jnp.float32),
        ],
        scratch_shapes=[pltpu.VMEM((turn + taps - 1, requests, BLOCK), jnp.float32)],
        compiler_params=pltpu.CompilerParams(vmem_limit_bytes=40 * 1024 * 1024),
        cost_estimate=pl.CostEstimate(
            flops=2 * rows * inner * cols,
            bytes_accessed=rows * inner * 4 + inner * cols * 2 + rows * cols * 4,
            transcendentals=2 * rows * inner,
        ),
    )(hidden_x, start, conv_weight, conv_bias.reshape(1, -1), x_weight)


def scan_kernel(
    aliased,
    norm_ref,
    x_ref,
    z_ref,
    dtw_ref,
    dtb_ref,
    alog_ref,
    skip_ref,
    state_ref,
    *rest,
):
    if aliased:
        rest = rest[1:]
    out_ref, final_ref, bc_s, dt_s, drive_s, y_s = rest
    step = pl.program_id(0)
    requests, turn, width = z_ref.shape
    states = alog_ref.shape[0]
    rank = dtw_ref.shape[0]
    rows = requests * turn
    tile = 128

    @pl.when(step == 0)
    def _():
        def spread(i, _):
            row = pl.multiple_of(i * 16, 16)
            both = norm_ref[pl.ds(row, 16), rank:].astype(jnp.float32)
            for half in range(16 // requests):
                part = both[half * requests : (half + 1) * requests]
                t = i * (16 // requests) + half
                for n in range(2 * states):
                    bc_s[t, n] = jnp.broadcast_to(part[:, n : n + 1], (requests, LANES))
            return 0

        lax.fori_loop(0, rows // 16, spread, 0)

    bias = dtb_ref[...]
    skip = skip_ref[...]

    def steps(i, _):
        row = pl.multiple_of(i * tile, tile)
        raw = jnp.dot(
            norm_ref[pl.ds(row, tile), :rank], dtw_ref[...], preferred_element_type=jnp.float32
        )
        raw = raw + bias
        dt = jnp.maximum(raw, 0.0) + jnp.log1p(jnp.exp(-jnp.abs(raw)))
        x = x_ref[pl.ds(row, tile), :].astype(jnp.float32)
        dt_s[pl.ds(row, tile), :] = dt
        drive_s[pl.ds(row, tile), :] = dt * x
        y_s[pl.ds(row, tile), :] = skip * x
        return 0

    lax.fori_loop(0, rows // tile, steps, 0)

    for part in range(width // LANES):
        lanes = slice(part * LANES, (part + 1) * LANES)
        rates = -jnp.exp(alog_ref[:, lanes]) * LOG2E
        rates = [jnp.broadcast_to(rates[n : n + 1], (requests, LANES)) for n in range(states)]
        start = jnp.swapaxes(state_ref[:, :, lanes].astype(jnp.float32), 0, 1)
        unroll = 4

        def advance(i, held):
            held = list(held)
            for k in range(unroll):
                t = i * unroll + k
                row = pl.ds(pl.multiple_of(t * requests, requests), requests)
                dt = dt_s[row, lanes]
                drive = drive_s[row, lanes]
                sums = [y_s[row, lanes], None, None, None]
                for n in range(states):
                    held[n] = jnp.exp2(dt * rates[n]) * held[n] + drive * bc_s[t, n]
                    term = held[n] * bc_s[t, states + n]
                    q = n % 4
                    sums[q] = term if sums[q] is None else sums[q] + term
                y_s[row, lanes] = (sums[0] + sums[1]) + (sums[2] + sums[3])
            return tuple(held)

        held = lax.fori_loop(
            0, turn // unroll, advance, tuple(start[n] for n in range(states))
        )
        final_ref[:, :, lanes] = jnp.swapaxes(jnp.stack(held), 0, 1)

    span = 16

    def gate(i, _):
        t = pl.multiple_of(i * span, span)
        row = pl.multiple_of(i * span * requests, span * requests)
        y = y_s[pl.ds(row, span * requests), :].reshape(span, requests, width)
        z = z_ref[:, pl.ds(t, span), :].astype(jnp.float32)
        out_ref[:, pl.ds(t, span), :] = (
            jnp.swapaxes(y, 0, 1) * (z / (1.0 + jnp.exp(-z)))
        ).astype(jnp.bfloat16)
        return 0

    lax.fori_loop(0, turn // span, gate, 0)


def scan_gate(
    chunk, turn, norm, conv_out, gate_z, dt_weight, dt_bias, a_log, skip_gain, state, gated
):
    requests, whole, inner = gate_z.shape
    states = a_log.shape[0]
    rank = dt_weight.shape[0]
    cols = norm.shape[1]
    rows = requests * turn
    vector = pl.BlockSpec((1, BLOCK), lambda j: (0, j))
    gate_spec = pl.BlockSpec((requests, turn, BLOCK), lambda j: (0, chunk, j))
    state_spec = pl.BlockSpec((requests, states, BLOCK), lambda j: (0, 0, j))
    in_specs = [
        pl.BlockSpec((rows, cols), lambda j: (0, 0)),
        pl.BlockSpec((rows, BLOCK), lambda j: (0, j)),
        gate_spec,
        pl.BlockSpec((rank, BLOCK), lambda j: (0, j)),
        vector,
        pl.BlockSpec((states, BLOCK), lambda j: (0, j)),
        vector,
        state_spec,
    ]
    args = [
        norm,
        conv_out,
        gate_z,
        dt_weight,
        dt_bias.reshape(1, -1),
        a_log,
        skip_gain.reshape(1, -1),
        state,
    ]
    aliases = {}
    if gated is not None:
        aliases = {len(args): 0}
        in_specs.append(pl.BlockSpec(memory_space=pl.ANY))
        args.append(gated)
    return pl.pallas_call(
        functools.partial(scan_kernel, gated is not None),
        grid=(inner // BLOCK,),
        in_specs=in_specs,
        out_specs=[gate_spec, state_spec],
        out_shape=[
            jax.ShapeDtypeStruct((requests, whole, inner), jnp.bfloat16),
            jax.ShapeDtypeStruct((requests, states, inner), jnp.float32),
        ],
        scratch_shapes=[
            pltpu.VMEM((turn, 2 * states, requests, LANES), jnp.float32),
            pltpu.VMEM((rows, BLOCK), jnp.float32),
            pltpu.VMEM((rows, BLOCK), jnp.float32),
            pltpu.VMEM((rows, BLOCK), jnp.float32),
        ],
        input_output_aliases=aliases,
        compiler_params=pltpu.CompilerParams(vmem_limit_bytes=48 * 1024 * 1024),
        cost_estimate=pl.CostEstimate(
            flops=2 * rows * inner * rank + 6 * rows * inner * states,
            bytes_accessed=rows * inner * 6 + rank * inner * 2,
            transcendentals=rows * inner * states,
        ),
    )(*args)


def body(
    hidden_x,
    gate_z,
    conv_weight,
    conv_bias,
    x_weight,
    dt_weight,
    dt_bias,
    a_log,
    skip_gain,
    ssm_cache,
    conv_cache,
    holder_of,
    slot_of,
):
    groups = lax.axis_size("dp")
    my_index = lax.axis_index("dp")
    requests, whole, _ = hidden_x.shape
    slot_count = ssm_cache.shape[0]
    capacity = slot_count // groups
    state_width = a_log.shape[0]
    rank_width = dt_weight.shape[0]
    kept_rows = conv_cache.shape[1]
    holders = holder_of.reshape(groups, requests)
    places = slot_of.reshape(groups, requests)
    earlier = jnp.arange(requests)[None, :] < jnp.arange(requests)[:, None]
    same_holder = holders[:, :, None] == holders[:, None, :]
    rank_within = jnp.sum((same_holder & earlier[None, :, :]).astype(jnp.int32), axis=2)
    rank_range = jnp.arange(capacity, dtype=jnp.int32)

    paired = groups & (groups - 1) == 0
    order = jnp.arange(groups, dtype=jnp.int32)
    if paired:
        sent_to = my_index ^ order
        came_from = sent_to
        pairs = [[(i, i ^ k) for i in range(groups)] for k in range(groups)]
    else:
        sent_to = (my_index + order) % groups
        came_from = (my_index - order) % groups
        pairs = [[(i, (i + k) % groups) for i in range(groups)] for k in range(groups)]

    def exchange(blocks):
        return [
            block if k == 0 else lax.ppermute(block, "dp", pairs[k])
            for k, block in enumerate(blocks)
        ]

    served = (holders == my_index)[:, None, :] & (
        rank_within[:, None, :] == rank_range[None, :, None]
    )
    occupied = jnp.any(served, axis=2)
    sources = jnp.sum(jnp.where(served, places[:, None, :], 0), axis=2)
    own_holders = holders[my_index]
    own_ranks = rank_within[my_index]
    if paired:
        own_steps = own_holders ^ my_index
    else:
        own_steps = (my_index - own_holders) % groups
    lookup = own_steps * capacity + own_ranks

    wanted = sources[sent_to]
    conv_rows = jnp.swapaxes(conv_cache[wanted.reshape(-1)], 0, 1)
    conv_rows = conv_rows.reshape((kept_rows, groups, capacity) + conv_rows.shape[2:])
    conv_got = exchange([conv_rows[:, k] for k in range(groups)])
    conv_start = jnp.concatenate(conv_got, axis=1)[:, lookup]

    ssm_rows = ssm_cache[wanted].astype(jnp.bfloat16)
    ssm_got = exchange([ssm_rows[k] for k in range(groups)])
    state = jnp.concatenate(ssm_got, axis=0)[lookup]

    own_placed = (own_holders[None, None, :] == sent_to[:, None, None]) & (
        own_ranks[None, None, :] == rank_range[None, :, None]
    )
    picked_rows = jnp.sum(
        jnp.where(own_placed, jnp.arange(requests, dtype=jnp.int32)[None, None, :], 0), axis=2
    )
    targets = jnp.where(occupied, sources, slot_count)[came_from].reshape(-1)

    last_inputs = hidden_x[:, whole - kept_rows :, :][picked_rows]
    last_got = exchange([last_inputs[k] for k in range(groups)])
    new_conv = conv_cache.at[targets].set(
        jnp.concatenate(last_got, axis=0).astype(jnp.float32), mode="drop"
    )

    turn = whole // CHUNKS
    conv_outs, norms = [], []
    for chunk in range(CHUNKS):
        if chunk == 0:
            start = conv_start
        else:
            start = jnp.swapaxes(
                hidden_x[:, chunk * turn - kept_rows : chunk * turn, :], 0, 1
            ).astype(jnp.float32)
        conv_out, projected = conv_project(
            chunk, turn, hidden_x, start, conv_weight, conv_bias, x_weight
        )
        share = lax.psum_scatter(projected, "tensor", scatter_dimension=0, tiled=True)
        norm_share = normalize(share, rank_width, state_width)
        conv_outs.append(conv_out)
        norms.append(lax.all_gather(norm_share, "tensor", axis=0, tiled=True))

    gated = None
    for chunk in range(CHUNKS):
        gated, state = scan_gate(
            chunk,
            turn,
            norms[chunk],
            conv_outs[chunk],
            gate_z,
            dt_weight,
            dt_bias,
            a_log,
            skip_gain,
            state,
            gated,
        )

    final_rows = state[picked_rows].astype(jnp.bfloat16)
    final_got = exchange([final_rows[k] for k in range(groups)])
    new_ssm = ssm_cache.at[targets].set(
        jnp.concatenate(final_got, axis=0).astype(jnp.float32), mode="drop"
    )
    return (gated, new_ssm, new_conv)


def solution(mesh):
    placed = (
        P("dp", None, "tensor"),
        P("dp", None, "tensor"),
        P(None, "tensor"),
        P("tensor"),
        P("tensor", None),
        P(None, "tensor"),
        P("tensor"),
        P(None, "tensor"),
        P("tensor"),
        P("dp", None, "tensor"),
        P("dp", None, "tensor"),
        P(),
        P(),
    )
    return jax.shard_map(
        body,
        mesh=mesh,
        in_specs=placed,
        out_specs=(P("dp", None, "tensor"), P("dp", None, "tensor"), P("dp", None, "tensor")),
        check_vma=False,
    )
```

time: 386 us -> 219 us (0.57)
  other arithmetic: 136 us -> 12 us
  local copies, waits for them, and re-layouts: 148 us -> 32.1 us
  Pallas kernels: 0 us -> 85.9 us
  blocking collectives: 13.2 us -> 31.7 us
  matrix products: 15.4 us -> 0 us
  waiting for transfers between devices: 36.2 us -> 26.2 us
    reduce_sum x49 -> x1, other arithmetic: 91.1 us -> 0.15 us  [body(): jnp.sum(jnp.where(own_placed, jnp.arange(requests, dtype=jnp.int32)[None,...]
    pallas_call x0 -> x4, Pallas kernels: none -> 85.9 us  [the longest x2 71.4 us: scan_gate(): pl.pallas_call(functools.partial(scan_kernel, gated is not None), grid=(i...]
    slice x18 -> x4, local copies, waits for them, and re-layouts: 83.4 us -> 2.04 us  [the longest x1 1.18 us: body(): last_inputs = hidden_x[:, whole - kept_rows:, :][picked_rows]]
    convert_element_type x4 -> x3, other arithmetic: 30.1 us -> 1.04 us  [the longest x1 0.87 us: body(): jnp.concatenate(last_got, axis=0).astype(jnp.float32)]
    all_gather x1 -> x2, blocking collectives: 13.2 us -> 31.7 us  [body(): norms.append(lax.all_gather(norm_share, 'tensor', axis=0, tiled=True))]
    dynamic_update_slice x16 -> x0, local copies, waits for them, and re-layouts: 17.5 us -> none  [recur_blocks(): lax.scan(one_block, state_start, (time_major(dt_full), time_major(drive_f...]
    all_to_all x4 -> x0, starting transfers between devices: 17.4 us -> none  [the longest x1 5.19 us: body(): lax.all_to_all(outgoing[1], 'dp', split_axis=0, concat_axis=0, tiled=True)]
    dot_general x2 -> x0, matrix products: 15.4 us -> none  [the longest x1 11.5 us: body(): jnp.dot(dt_norm, dt_weight, preferred_element_type=jnp.float32)]
  transfers between devices with their start and end apart: 6 -> 14, of which waited for: 2 -> 5; matrix products, arithmetic and copies ran while one was open for 8% -> 12% of each run, Pallas kernels for 0% -> 39%
where the time goes in v1:
time: 219 us; the launch traced here: 218 us
  Pallas kernels  85.9 us (39%)
  local copies, waits for them, and re-layouts  32.1 us (15%)
  blocking collectives  31.7 us (14%)
  waiting for transfers between devices  26.2 us (12%)
  starting transfers between devices  15.3 us (7%)
  between operations  14.5 us (7%)
  other arithmetic  12 us (5%)
    pallas_call x2, Pallas kernels, scan_gate(): pl.pallas_call(functools.partial(scan_kernel, gated is not None), grid=(i...  71.4 us
    all_gather x2, blocking collectives, body(): norms.append(lax.all_gather(norm_share, 'tensor', axis=0, tiled=True))  31.7 us
    reduce_scatter x2, waiting for transfers between devices, body(): lax.psum_scatter(projected, 'tensor', scatter_dimension=0, tiled=True)  21.2 us
    unnamed x51, local copies, waits for them, and re-layouts  17.9 us
    ppermute x12, starting transfers between devices, exchange(): lax.ppermute(block, 'dp', pairs[k])  15.2 us
    pallas_call x2, Pallas kernels, conv_project(): pl.pallas_call(conv_kernel, grid=(inner // BLOCK,), in_specs=[pl.BlockSpe...  14.5 us
    ppermute x12, waiting for transfers between devices, exchange(): lax.ppermute(block, 'dp', pairs[k])  4.91 us
  transfers between devices with their start and end apart: 14, of which 5 were waited for; matrix products, arithmetic and copies ran while one was open for 12% of the time, Pallas kernels for 39%

profile of v1, /device:TPU:0, one launch (start us, length us, event | category | flops | bytes accessed | tf_op | source)
XLA Modules:
  0.0 217.8 jit_solution(13637641287048777133)
XLA Ops:
  7.2 0.9 copy.101
  8.1 2.4 %copy.100 = f32[8,16,2048]{2,1,0:T(8,128)} copy(f32[8,16,2048]{2,1,0:T(8,128)} %param.22) | data formatting | bytes 2097152
  10.5 0.7 reshape.296
  11.3 0.2 convert_reduce_fusion
  11.5 0.7 broadcast_in_dim.21
  12.2 0.1 select_reduce_fusion.1
  12.5 0.6 gather_fusion
  13.1 0.8 gather_fusion.1
  14.0 0.1 copy.86
  14.1 0.7 slice_bitcast_fusion.3
  14.8 3.9 %collective-permute-start.2 = (f32[3,2,2048]{2,0,1:T(4,128)}, f32[3,2,2048]{2,0,1:T(4,128)S(1)}, u32[]{:S(2)}, u32[]{:S(2)}) collective-permute-start(f32[3,2,2048]{2,0,1:T(4,128)} %get-tuple-element.34), channel_id=1, source_target_pairs={{0,24},{8,16},{16,8},{24,0},{1,25},{9,17},{17,9},{25,1},{2,26},{10... | collective-permute-start | bytes 147464 | tf_op jit(solution)/shard_map/ppermute | solution.py:306
  18.8 0.5 collective-permute-start.1
  19.3 1.2 fusion.8
  20.6 3.1 %copy.69.xw_ref = bf16[2048,544]{1,0:T(8,128)(2,1)S(1)} copy(bf16[2048,544]{0,1:T(8,128)(2,1)} %param.17) | data formatting | bytes 4456448 | tf_op args[4]
  23.7 2.2 %copy-done = bf16[8,128,2048]{2,1,0:T(8,128)(2,1)S(1)} copy-done((bf16[8,128,2048]{2,1,0:T(8,128)(2,1)S(1)}, bf16[8,128,2048]{2,1,0:T(8,128)(2,1)}, u32[]{:S(2)}) %copy-start) | copy-done | bytes 4194328
  25.9 7.3 %shard_map.148 = (bf16[512,2048]{1,0:T(8,128)(2,1)S(1)}, f32[512,544]{1,0:T(8,128)S(1)}) custom-call(bf16[8,128,2048]{2,1,0:T(8,128)(2,1)S(1)} %copy-done, f32[3,8,2048]{2,1,0:T(8,128)S(1)} %convert_bitcast_fusion.start_ref, f32[4,2048]{1,0:T(4,128)S(1)} %copy-done.4, f32[1,2048]{1,0:T(1,128)S(1)} %bitcast.43, bf16[2048,544]{1,0:T(8,128)(2,1)S(1)} %copy.69.xw_ref), custom_call_target="tpu_custom_call" | custom-call | flops 1140850688 | bytes 7536640 | tf_op jit(solution)/shard_map/pallas_call | solution.py:77
  33.2 1.1 copy-done.2
  34.3 1.3 copy-done.6
  35.8 0.1 select_reduce_fusion
  36.1 0.7 gather_fusion.7
  36.8 0.6 copy.91
  37.5 2.9 %collective-permute-start.11 = (bf16[2,3,2048]{2,0,1:T(2,128)(2,1)}, bf16[2,3,2048]{2,0,1:T(2,128)(2,1)S(1)}, u32[]{:S(2)}, u32[]{:S(2)}) collective-permute-start(bf16[2,3,2048]{2,0,1:T(2,128)(2,1)} %copy.91), channel_id=1, source_target_pairs={{0,24},{8,16},{16,8},{24,0},{1,25},{9,17},{17,9},{25,1},{2,26},{10... | collective-permute-start | bytes 73736 | tf_op jit(solution)/shard_map/ppermute | solution.py:306
  40.4 0.6 copy.89
  41.0 0.5 collective-permute-start.9
  41.9 1.8 gather_fusion.3
  43.7 0.8 fusion.10
  44.5 1.6 collective-permute-start.3
  46.1 2.0 collective-permute-start.4
  48.1 0.9 pad_maximum_fusion.1
  49.0 0.7 gather_fusion.2
  49.9 2.2 %copy-done.1 = bf16[8,128,2048]{2,1,0:T(8,128)(2,1)S(1)} copy-done((bf16[8,128,2048]{2,1,0:T(8,128)(2,1)S(1)}, bf16[8,128,2048]{2,1,0:T(8,128)(2,1)}, u32[]{:S(2)}) %copy-start.1) | copy-done | bytes 4194328
  52.1 7.3 %shard_map.149 = (bf16[512,2048]{1,0:T(8,128)(2,1)S(1)}, f32[512,544]{1,0:T(8,128)S(1)}) custom-call(bf16[8,128,2048]{2,1,0:T(8,128)(2,1)S(1)} %copy-done.1, f32[3,8,2048]{2,1,0:T(8,128)S(1)} %bitcast.42, f32[4,2048]{1,0:T(4,128)S(1)} %copy-done.4, f32[1,2048]{1,0:T(1,128)S(1)} %bitcast.44, bf16[2048,544]{1,0:T(8,128)(2,1)S(1)} %copy.69.xw_ref), custom_call_target="tpu_custom_call" | custom-call | flops 1140850688 | bytes 7536640 | tf_op jit(solution)/shard_map/pallas_call | solution.py:77
  59.4 1.1 copy-done.3
  60.4 1.3 copy-done.8
  61.8 0.1 fusion.1
  62.1 0.8 gather_fusion.5
  63.1 0.2 collective-permute-start.10
  63.3 1.1 pad_maximum_fusion
  64.4 0.7 gather_fusion.4
  65.1 5.7 %reduce-scatter.3.cloned.1.call-done = f32[64,544]{1,0:T(8,128)} async-done(((f32[512,544]{1,0:T(8,128)}), f32[64,544]{1,0:T(8,128)}) %reduce-scatter.3.cloned.1.call-update) | async-done | bytes 139280 | tf_op jit(solution)/shard_map/reduce_scatter | solution.py:359
  70.8 1.0 multiply_reduce_fusion.5
  71.8 1.0 multiply_reduce_fusion.1
  72.8 0.9 multiply_convert_fusion.5
  73.8 1.0 multiply_convert_fusion.1
  74.8 16.5 %all_gather.6.norm_ref = bf16[512,544]{1,0:T(8,128)(2,1)S(1)} all-gather(bf16[64,544]{1,0:T(8,128)(2,1)S(1)} %pad_maximum_fusion.2), channel_id=1, replica_groups=mesh['dp'=4,'tensor'=8] {'tensor'}, dimensions={0}, use_global_device_ids=true | all-gather | bytes 626688 | tf_op jit(solution)/shard_map/all_gather | solution.py:362
  91.4 15.5 %reduce-scatter.5.cloned.1.call-done = f32[64,544]{1,0:T(8,128)} async-done(((f32[512,544]{1,0:T(8,128)}), f32[64,544]{1,0:T(8,128)}) %reduce-scatter.5.cloned.1.call-update) | async-done | bytes 139280 | tf_op jit(solution)/shard_map/reduce_scatter | solution.py:359
  106.9 1.0 multiply_reduce_fusion
  108.0 1.0 multiply_reduce_fusion.3
  109.0 1.0 multiply_convert_fusion
  110.0 0.9 multiply_convert_fusion.3
  111.0 15.2 %all_gather.7.norm_ref = bf16[512,544]{1,0:T(8,128)(2,1)S(1)} all-gather(bf16[64,544]{1,0:T(8,128)(2,1)S(1)} %pad_maximum_fusion.3), channel_id=1, replica_groups=mesh['dp'=4,'tensor'=8] {'tensor'}, dimensions={0}, use_global_device_ids=true | all-gather | bytes 626688 | tf_op jit(solution)/shard_map/all_gather | solution.py:362
  126.2 35.8 %shard_map.150 = (bf16[8,128,2048]{2,1,0:T(8,128)(2,1)}, f32[8,16,2048]{2,1,0:T(8,128)S(1)}) custom-call(bf16[512,544]{1,0:T(8,128)(2,1)S(1)} %all_gather.7.norm_ref, bf16[512,2048]{1,0:T(8,128)(2,1)S(1)} %copy-done.9, bf16[8,128,2048]{2,1,0:T(8,128)(2,1)} %z_ref.3, bf16[512,2048]{1,0:T(8,128)(2,1)} %dtw_ref.3, f32[1,2048]{1,0:T(1,128)S(1)} %bitcast.45, ...), custom_call_target="tpu_custom_call" | custom-call | flops 1174405120 | bytes 8388608 | tf_op jit(solution)/shard_map/pallas_call | solution.py:238
  162.0 35.6 %shard_map.151 = (bf16[8,128,2048]{2,1,0:T(8,128)(2,1)}, f32[8,16,2048]{2,1,0:T(8,128)S(1)}) custom-call(bf16[512,544]{1,0:T(8,128)(2,1)S(1)} %all_gather.6.norm_ref, bf16[512,2048]{1,0:T(8,128)(2,1)S(1)} %copy-done.7, bf16[8,128,2048]{2,1,0:T(8,128)(2,1)} %z_ref.3, bf16[512,2048]{1,0:T(8,128)(2,1)} %dtw_ref.3, ...), custom_call_target="tpu_custom_call", output_to_operand_aliasing={{0}: (8, {})} | custom-call | flops 1174405120 | bytes 8388608 | tf_op jit(solution)/shard_map/pallas_call | solution.py:238
  197.6 0.6 gather_fusion.6
  198.3 1.1 collective-permute-start.6
  199.4 1.6 collective-permute-start.8
  201.0 0.9 collective-permute-start.7
  201.9 0.9 maximum_convert_fusion.1
  202.7 1.3 scatter_fusion.1
  204.1 0.6 collective-permute-done.6
  204.7 2.9 %collective-permute-done.8 = bf16[2,16,2048]{2,1,0:T(8,128)(2,1)S(1)} collective-permute-done((bf16[2,16,2048]{2,1,0:T(8,128)(2,1)S(1)}, bf16[2,16,2048]{2,1,0:T(8,128)(2,1)S(1)}, u32[]{:S(2)}, u32[]{:S(2)}) %collective-permute-start.8) | collective-permute-done | bytes 131104 | tf_op jit(solution)/shard_map/ppermute | solution.py:306
  207.6 1.4 collective-permute-done.7
  209.1 0.9 scatter_fusion
  210.0 1.0 copy-done.17
  (92 shorter events, 2.0 us)
Async XLA Ops:
  7.2 63.6 %reduce-scatter.3.cloned.1.call-start = ((), (), s32[]{:S(2)}) async-start(), calls=%async_computation.2 | async-start | bytes 1474560 | tf_op jit(solution)/shard_map/reduce_scatter | solution.py:359
  8.1 6.7 %copy-start.13 = (f32[8,3,2048]{2,0,1:T(8,128)}, f32[8,3,2048]{2,0,1:T(8,128)S(1)}, u32[]{:S(2)}) copy-start(f32[8,3,2048]{2,0,1:T(8,128)S(1)} %copy.101) | copy-start | bytes 589828
  11.3 1.9 copy-start.20
  12.5 11.2 %copy-start.19 = (s32[1024]{0:T(1024)}, s32[1024]{0:T(1024)S(1)}, u32[]{:S(2)}) copy-start(s32[1024]{0:T(1024)S(1)} %pad_clamp_fusion.4) | copy-start | bytes 12292
  14.8 29.7 %collective-permute-start.2 = (f32[3,2,2048]{2,0,1:T(4,128)}, f32[3,2,2048]{2,0,1:T(4,128)S(1)}, u32[]{:S(2)}, u32[]{:S(2)}) collective-permute-start(f32[3,2,2048]{2,0,1:T(4,128)} %get-tuple-element.34), channel_id=1, source_target_pairs={{0,24},{8,16},{16,8},{24,0},{1,25},{9,17},{17,9},{25,1},{2,26},{10... | collective-permute-start | bytes 147464 | tf_op jit(solution)/shard_map/ppermute | solution.py:306
  18.8 27.3 %collective-permute-start.1 = (f32[3,2,2048]{2,0,1:T(4,128)}, f32[3,2,2048]{2,0,1:T(4,128)}, u32[]{:S(2)}, u32[]{:S(2)}) collective-permute-start(f32[3,2,2048]{2,0,1:T(4,128)} %get-tuple-element.35), channel_id=1, source_target_pairs={{0,16},{8,24},{16,0},{24,8},{1,17},{9,25},{17,1},{25,9},{2,18},{10... | collective-permute-start | bytes 147464 | tf_op jit(solution)/shard_map/ppermute | solution.py:306
  19.3 26.8 %collective-permute-start = (f32[3,2,2048]{2,0,1:T(4,128)}, f32[3,2,2048]{2,0,1:T(4,128)}, u32[]{:S(2)}, u32[]{:S(2)}) collective-permute-start(f32[3,2,2048]{2,0,1:T(4,128)} %get-tuple-element.36), channel_id=1, source_target_pairs={{0,8},{8,0},{16,24},{24,16},{1,9},{9,1},{17,25},{25,17},{2,10},{10... | collective-permute-start | bytes 147464 | tf_op jit(solution)/shard_map/ppermute | solution.py:306
  20.5 3.2 %copy-start.4 = (f32[4,2048]{1,0:T(4,128)S(1)}, f32[4,2048]{1,0:T(4,128)}, u32[]{:S(2)}) copy-start(f32[4,2048]{1,0:T(4,128)} %cw_ref.3) | copy-start | bytes 98308
  20.5 3.2 %copy-start.5 = (f32[2048]{0:T(1024)S(1)}, f32[2048]{0:T(1024)}, u32[]{:S(2)}) copy-start(f32[2048]{0:T(1024)} %param.16) | copy-start | bytes 24580
  23.7 2.2 %copy-start = (bf16[8,128,2048]{2,1,0:T(8,128)(2,1)S(1)}, bf16[8,128,2048]{2,1,0:T(8,128)(2,1)}, u32[]{:S(2)}) copy-start(bf16[8,128,2048]{2,1,0:T(8,128)(2,1)} %x_ref.3) | copy-start | bytes 12582916
  33.2 1.1 copy-start.2
  34.2 1.3 copy-start.6
  35.6 71.3 %reduce-scatter.5.cloned.1.call-start = ((), (), s32[]{:S(2)}) async-start(), calls=%async_computation.3 | async-start | bytes 1474560 | tf_op jit(solution)/shard_map/reduce_scatter | solution.py:359
  37.5 163.5 %collective-permute-start.11 = (bf16[2,3,2048]{2,0,1:T(2,128)(2,1)}, bf16[2,3,2048]{2,0,1:T(2,128)(2,1)S(1)}, u32[]{:S(2)}, u32[]{:S(2)}) collective-permute-start(bf16[2,3,2048]{2,0,1:T(2,128)(2,1)} %copy.91), channel_id=1, source_target_pairs={{0,24},{8,16},{16,8},{24,0},{1,25},{9,17},{17,9},{25,1},{2,26},{10... | collective-permute-start | bytes 73736 | tf_op jit(solution)/shard_map/ppermute | solution.py:306
  41.0 160.8 %collective-permute-start.9 = (bf16[2,3,2048]{2,0,1:T(2,128)(2,1)}, bf16[2,3,2048]{2,0,1:T(2,128)(2,1)}, u32[]{:S(2)}, u32[]{:S(2)}) collective-permute-start(bf16[2,3,2048]{2,0,1:T(2,128)(2,1)} %copy.89), channel_id=1, source_target_pairs={{0,8},{8,0},{16,24},{24,16},{1,9},{9,1},{17,25},{25,17},{2,10},{10... | collective-permute-start | bytes 73736 | tf_op jit(solution)/shard_map/ppermute | solution.py:306
  44.5 14.9 %copy-start.18 = (s32[1024]{0:T(1024)}, s32[1024]{0:T(1024)S(1)}, u32[]{:S(2)}) copy-start(s32[1024]{0:T(1024)S(1)} %pad_clamp_fusion.2) | copy-start | bytes 12292
  44.5 18.6 %collective-permute-start.3 = (bf16[2,16,2048]{2,1,0:T(8,128)(2,1)}, bf16[2,16,2048]{2,1,0:T(8,128)(2,1)}, u32[]{:S(2)}, u32[]{:S(2)}) collective-permute-start(bf16[2,16,2048]{2,1,0:T(8,128)(2,1)} %get-tuple-element.30), channel_id=1, source_target_pairs={{0,8},{8,0},{16,24},{24,16},{1,9},{9,1},{17,25},{25,17},{2,10},{10... | collective-permute-start | bytes 393224 | tf_op jit(solution)/shard_map/ppermute | solution.py:306
  46.1 17.2 %collective-permute-start.5 = (bf16[2,16,2048]{2,1,0:T(8,128)(2,1)}, bf16[2,16,2048]{2,1,0:T(8,128)(2,1)}, u32[]{:S(2)}, u32[]{:S(2)}) collective-permute-start(bf16[2,16,2048]{2,1,0:T(8,128)(2,1)} %get-tuple-element.31), channel_id=1, source_target_pairs={{0,24},{8,16},{16,8},{24,0},{1,25},{9,17},{17,9},{25,1},{2,26},{10... | collective-permute-start | bytes 393224 | tf_op jit(solution)/shard_map/ppermute | solution.py:306
  46.1 17.2 %collective-permute-start.4 = (bf16[2,16,2048]{2,1,0:T(8,128)(2,1)}, bf16[2,16,2048]{2,1,0:T(8,128)(2,1)}, u32[]{:S(2)}, u32[]{:S(2)}) collective-permute-start(bf16[2,16,2048]{2,1,0:T(8,128)(2,1)} %get-tuple-element.32), channel_id=1, source_target_pairs={{0,16},{8,24},{16,0},{24,8},{1,17},{9,25},{17,1},{25,9},{2,18},{10... | collective-permute-start | bytes 393224 | tf_op jit(solution)/shard_map/ppermute | solution.py:306
  49.9 2.2 %copy-start.1 = (bf16[8,128,2048]{2,1,0:T(8,128)(2,1)S(1)}, bf16[8,128,2048]{2,1,0:T(8,128)(2,1)}, u32[]{:S(2)}) copy-start(bf16[8,128,2048]{2,1,0:T(8,128)(2,1)} %x_ref.3) | copy-start | bytes 12582916
  52.1 9.7 %copy-start.21 = (pred[4,8]{1,0:T(4,128)(4,1)S(1)}, pred[4,8]{1,0:T(4,128)(4,1)}, u32[]{:S(2)}) copy-start(pred[4,8]{1,0:T(4,128)(4,1)} %copy-done.20) | copy-start | bytes 100
  59.4 1.1 copy-start.3
  60.4 1.3 copy-start.8
  61.8 64.4 %copy-start.9 = (bf16[512,2048]{1,0:T(8,128)(2,1)S(1)}, bf16[512,2048]{1,0:T(8,128)(2,1)}, u32[]{:S(2)}) copy-start(bf16[512,2048]{1,0:T(8,128)(2,1)} %copy-done.8) | copy-start | bytes 6291460
  61.8 64.4 %copy-start.10 = (f32[16,2048]{1,0:T(8,128)S(1)}, f32[16,2048]{1,0:T(8,128)}, u32[]{:S(2)}) copy-start(f32[16,2048]{1,0:T(8,128)} %alog_ref.3) | copy-start | bytes 393220
  61.8 64.4 %copy-start.11 = (f32[2048]{0:T(1024)S(1)}, f32[2048]{0:T(1024)}, u32[]{:S(2)}) copy-start(f32[2048]{0:T(1024)} %param.19) | copy-start | bytes 24580
  61.8 64.4 %copy-start.12 = (f32[2048]{0:T(1024)S(1)}, f32[2048]{0:T(1024)}, u32[]{:S(2)}) copy-start(f32[2048]{0:T(1024)} %param.21) | copy-start | bytes 24580
  63.1 138.7 %collective-permute-start.10 = (bf16[2,3,2048]{2,0,1:T(2,128)(2,1)S(1)}, bf16[2,3,2048]{2,0,1:T(2,128)(2,1)}, u32[]{:S(2)}, u32[]{:S(2)}) collective-permute-start(bf16[2,3,2048]{2,0,1:T(2,128)(2,1)S(1)} %copy.90), channel_id=1, source_target_pairs={{0,16},{8,24},{16,0},{24,8},{1,17},{9,25},{17,1},{25,9},{2,18},{10... | collective-permute-start | bytes 73736 | tf_op jit(solution)/shard_map/ppermute | solution.py:306
  126.2 35.8 %copy-start.7 = (bf16[512,2048]{1,0:T(8,128)(2,1)S(1)}, bf16[512,2048]{1,0:T(8,128)(2,1)}, u32[]{:S(2)}) copy-start(bf16[512,2048]{1,0:T(8,128)(2,1)} %copy-done.6) | copy-start | bytes 6291460
  197.6 5.1 %copy-start.14 = (f32[8,3,2048]{2,0,1:T(8,128)S(1)}, f32[8,3,2048]{2,0,1:T(8,128)}, u32[]{:S(2)}) copy-start(f32[8,3,2048]{2,0,1:T(8,128)} %copy-done.13) | copy-start | bytes 589828
  198.3 6.4 %collective-permute-start.6 = (bf16[2,16,2048]{2,1,0:T(8,128)(2,1)S(1)}, bf16[2,16,2048]{2,1,0:T(8,128)(2,1)S(1)}, u32[]{:S(2)}, u32[]{:S(2)}) collective-permute-start(bf16[2,16,2048]{2,1,0:T(8,128)(2,1)S(1)} %get-tuple-element.26), channel_id=1, source_target_pairs={{0,8},{8,0},{16,24},{24,16},{1,9},{9,1},{17,25},{25,17},{2,10},{10... | collective-permute-start | bytes 393224 | tf_op jit(solution)/shard_map/ppermute | solution.py:306
  199.4 8.2 %collective-permute-start.8 = (bf16[2,16,2048]{2,1,0:T(8,128)(2,1)S(1)}, bf16[2,16,2048]{2,1,0:T(8,128)(2,1)S(1)}, u32[]{:S(2)}, u32[]{:S(2)}) collective-permute-start(bf16[2,16,2048]{2,1,0:T(8,128)(2,1)S(1)} %get-tuple-element.27), channel_id=1, source_target_pairs={{0,24},{8,16},{16,8},{24,0},{1,25},{9,17},{17,9},{25,1},{2,26},{10... | collective-permute-start | bytes 393224 | tf_op jit(solution)/shard_map/ppermute | solution.py:306
  201.0 8.0 %collective-permute-start.7 = (bf16[2,16,2048]{2,1,0:T(8,128)(2,1)S(1)}, bf16[2,16,2048]{2,1,0:T(8,128)(2,1)S(1)}, u32[]{:S(2)}, u32[]{:S(2)}) collective-permute-start(bf16[2,16,2048]{2,1,0:T(8,128)(2,1)S(1)} %get-tuple-element.28), channel_id=1, source_target_pairs={{0,16},{8,24},{16,0},{24,8},{1,17},{9,25},{17,1},{25,9},{2,18},{10... | collective-permute-start | bytes 393224 | tf_op jit(solution)/shard_map/ppermute | solution.py:306
  202.7 6.3 %copy-start.16 = (f32[8,16,2048]{2,1,0:T(8,128)S(1)}, f32[8,16,2048]{2,1,0:T(8,128)}, u32[]{:S(2)}) copy-start(f32[8,16,2048]{2,1,0:T(8,128)} %copy.100) | copy-start | bytes 3145732
  204.1 5.9 %copy-start.15 = (f32[8,3,2048]{2,0,1:T(8,128)}, f32[8,3,2048]{2,0,1:T(8,128)S(1)}, u32[]{:S(2)}) copy-start(f32[8,3,2048]{2,0,1:T(8,128)S(1)} %scatter_fusion.1) | copy-start | bytes 589828
  209.9 1.0 copy-start.17
Sparse Core Ops, SparseCore 0:
  35.7 35.0 reduce-scatter.2
  73.1 33.8 reduce-scatter.4

commit v2 on v1

--- a/solution.py
+++ b/solution.py
@@ -10,23 +10,152 @@
 EPSILON = 1e-06
 NORM_FLOOR = 0.25
 LOG2E = 1.4426950408889634
-CHUNKS = 2
+CHUNKS = 1
 BLOCK = 256
 LANES = 128
 
 
-def normalize(projected, rank_width, state_width):
-    dt_raw = projected[:, :rank_width]
-    inject_raw = projected[:, rank_width : rank_width + state_width]
-    readout_raw = projected[:, rank_width + state_width :]
-    dt_norm = dt_raw * lax.rsqrt(jnp.mean(dt_raw * dt_raw, axis=1, keepdims=True) + EPSILON)
-    inject_norm = inject_raw * lax.rsqrt(
-        jnp.maximum(jnp.mean(inject_raw * inject_raw, axis=1, keepdims=True), NORM_FLOOR)
-    )
-    readout_norm = readout_raw * lax.rsqrt(
-        jnp.maximum(jnp.mean(readout_raw * readout_raw, axis=1, keepdims=True), NORM_FLOOR)
-    )
-    return jnp.concatenate([dt_norm, inject_norm, readout_norm], axis=1).astype(jnp.bfloat16)
+def silu(value):
+    return (0.5 * value) * (1.0 + jnp.tanh(0.5 * value))
+
+
+def softplus(value):
+    small = jnp.exp(-jnp.abs(value))
+    series = small * (1.0 - small * (0.5 - small * (1.0 / 3.0 - small * 0.25)))
+    return jnp.maximum(value, 0.0) + jnp.where(small < 0.0078125, series, jnp.log(1.0 + small))
+
+
+def reduce_kernel(
+    rank,
+    states,
+    proj_ref,
+    out_ref,
+    pair_s,
+    send_s,
+    recv_s,
+    total_s,
+    mine_s,
+    near_s,
+    far_s,
+    pair_send,
+    pair_recv,
+    sum_send,
+    sum_recv,
+    near_send,
+    near_recv,
+    far_send,
+    far_recv,
+):
+    chips, share, cols = pair_s.shape
+    me = lax.axis_index("tensor")
+    core = lax.rem(me, 2)
+    chip = lax.div(me, 2)
+    partner = chip * 2 + (1 - core)
+
+    def chip_at(offset):
+        return lax.rem(chip + offset, chips)
+
+    def block(owner):
+        return pl.ds(pl.multiple_of(owner * share, share), share)
+
+    def remote(src, dst, send, recv, target):
+        copy = pltpu.make_async_remote_copy(
+            src_ref=src,
+            dst_ref=dst,
+            send_sem=send,
+            recv_sem=recv,
+            device_id={"tensor": target},
+            device_id_type=pl.DeviceIdType.MESH,
+        )
+        copy.start()
+        return copy
+
+    barrier = pltpu.get_barrier_semaphore()
+    peers = [partner] + [chip_at(o) * 2 + core for o in range(1, chips)]
+    for peer in peers:
+        pl.semaphore_signal(
+            barrier, inc=1, device_id={"tensor": peer}, device_id_type=pl.DeviceIdType.MESH
+        )
+    pl.semaphore_wait(barrier, chips)
+
+    pairs, sums, nears, fars = {}, {}, {}, {}
+    for o in list(range(1, chips)) + [0]:
+        owner = chip_at(o) * 2 + (1 - core)
+        pairs[o] = remote(
+            proj_ref.at[block(owner)], pair_s.at[o], pair_send.at[o], pair_recv.at[o], partner
+        )
+    for o in range(1, chips):
+        owner = chip_at(o) * 2 + core
+        pairs[o].wait_recv()
+        send_s[o] = (proj_ref[block(owner), :] + pair_s[o]).astype(jnp.bfloat16)
+        sums[o] = remote(send_s.at[o], recv_s.at[o], sum_send.at[o], sum_recv.at[o], owner)
+    pairs[0].wait_recv()
+    total_s[...] = proj_ref[block(me), :] + pair_s[0]
+    for o in range(1, chips):
+        sums[o].wait_recv()
+        total_s[...] += recv_s[o].astype(jnp.float32)
+
+    head = total_s[:, :rank]
+    mean = jnp.sum(head * head, axis=1, keepdims=True) / rank
+    mine_s[:, :rank] = (head * lax.rsqrt(mean + EPSILON)).astype(jnp.bfloat16)
+    tail = total_s[:, rank:]
+    square = tail * tail
+    inject = lax.broadcasted_iota(jnp.int32, tail.shape, 1) < states
+    first = jnp.sum(jnp.where(inject, square, 0.0), axis=1, keepdims=True) / states
+    second = jnp.sum(jnp.where(inject, 0.0, square), axis=1, keepdims=True) / states
+    scale = jnp.where(
+        inject,
+        lax.rsqrt(jnp.maximum(first, NORM_FLOOR)),
+        lax.rsqrt(jnp.maximum(second, NORM_FLOOR)),
+    )
+    mine_s[:, rank:] = (tail * scale).astype(jnp.bfloat16)
+
+    for o in range(1, chips):
+        nears[o] = remote(
+            mine_s, near_s.at[o], near_send.at[o], near_recv.at[o], chip_at(o) * 2 + core
+        )
+    fars[0] = remote(mine_s, far_s.at[0], far_send.at[0], far_recv.at[0], partner)
+    out_ref[block(me), :] = mine_s[...]
+    for o in range(1, chips):
+        nears[o].wait_recv()
+        fars[o] = remote(near_s.at[o], far_s.at[o], far_send.at[o], far_recv.at[o], partner)
+        out_ref[block(chip_at(chips - o) * 2 + core), :] = near_s[o]
+    for o in range(chips):
+        fars[o].wait_recv()
+        out_ref[block(chip_at(chips - o) * 2 + (1 - core)), :] = far_s[o]
+    for group in (pairs, sums, nears, fars):
+        for copy in group.values():
+            copy.wait_send()
+
+
+def reduce_norm(projected, rank, states):
+    rows, cols = projected.shape
+    devices = lax.axis_size("tensor")
+    chips = devices // 2
+    share = rows // devices
+    shape = (chips, share, cols)
+    return pl.pallas_call(
+        functools.partial(reduce_kernel, rank, states),
+        in_specs=[pl.BlockSpec(memory_space=pltpu.VMEM)],
+        out_specs=pl.BlockSpec(memory_space=pltpu.VMEM),
+        out_shape=jax.ShapeDtypeStruct((rows, cols), jnp.bfloat16),
+        scratch_shapes=[
+            pltpu.VMEM(shape, jnp.float32),
+            pltpu.VMEM(shape, jnp.bfloat16),
+            pltpu.VMEM(shape, jnp.bfloat16),
+            pltpu.VMEM(shape[1:], jnp.float32),
+            pltpu.VMEM(shape[1:], jnp.bfloat16),
+            pltpu.VMEM(shape, jnp.bfloat16),
+            pltpu.VMEM(shape, jnp.bfloat16),
+        ]
+        + [pltpu.SemaphoreType.DMA((chips,))] * 8,
+        compiler_params=pltpu.CompilerParams(
+            collective_id=1, has_side_effects=True, vmem_limit_bytes=24 * 1024 * 1024
+        ),
+        cost_estimate=pl.CostEstimate(
+            flops=rows * cols * 4, bytes_accessed=40000000, transcendentals=0
+        ),
+    )(projected)
 
 
 def conv_kernel(x_ref, start_ref, cw_ref, cb_ref, xw_ref, out_ref, proj_ref, ext):
@@ -51,7 +180,7 @@
         total = ext[pl.ds(t, tile)] * weights[0] + bias
         for j in range(1, taps):
             total = total + ext[pl.ds(t + j, tile)] * weights[j]
-        value = total / (1.0 + jnp.exp(-total))
+        value = silu(total)
         row = pl.multiple_of(t * requests, tile * requests)
         out_ref[pl.ds(row, tile * requests), :] = value.reshape(tile * requests, width).astype(
             jnp.bfloat16
@@ -147,7 +276,7 @@
             norm_ref[pl.ds(row, tile), :rank], dtw_ref[...], preferred_element_type=jnp.float32
         )
         raw = raw + bias
-        dt = jnp.maximum(raw, 0.0) + jnp.log1p(jnp.exp(-jnp.abs(raw)))
+        dt = softplus(raw)
         x = x_ref[pl.ds(row, tile), :].astype(jnp.float32)
         dt_s[pl.ds(row, tile), :] = dt
         drive_s[pl.ds(row, tile), :] = dt * x
@@ -161,7 +290,7 @@
         rates = -jnp.exp(alog_ref[:, lanes]) * LOG2E
         rates = [jnp.broadcast_to(rates[n : n + 1], (requests, LANES)) for n in range(states)]
         start = jnp.swapaxes(state_ref[:, :, lanes].astype(jnp.float32), 0, 1)
-        unroll = 4
+        unroll = 8
 
         def advance(i, held):
             held = list(held)
@@ -192,7 +321,7 @@
         y = y_s[pl.ds(row, span * requests), :].reshape(span, requests, width)
         z = z_ref[:, pl.ds(t, span), :].astype(jnp.float32)
         out_ref[:, pl.ds(t, span), :] = (
-            jnp.swapaxes(y, 0, 1) * (z / (1.0 + jnp.exp(-z)))
+            jnp.swapaxes(y, 0, 1) * silu(z)
         ).astype(jnp.bfloat16)
         return 0
 
@@ -356,10 +485,8 @@
         conv_out, projected = conv_project(
             chunk, turn, hidden_x, start, conv_weight, conv_bias, x_weight
         )
-        share = lax.psum_scatter(projected, "tensor", scatter_dimension=0, tiled=True)
-        norm_share = normalize(share, rank_width, state_width)
         conv_outs.append(conv_out)
-        norms.append(lax.all_gather(norm_share, "tensor", axis=0, tiled=True))
+        norms.append(reduce_norm(projected, rank_width, state_width))
 
     gated = None
     for chunk in range(CHUNKS):

time: 219 us -> 163 us (0.74)
  blocking collectives: 31.7 us -> 0 us
  Pallas kernels: 85.9 us -> 110 us
  waiting for transfers between devices: 26.2 us -> 4.76 us
  between operations: 14.5 us -> 0.99 us
  other arithmetic: 12 us -> 3.78 us
  local copies, waits for them, and re-layouts: 32.1 us -> 25.1 us
    pallas_call x0 -> x1, Pallas kernels: none -> 32.6 us  [reduce_norm(): pl.pallas_call(functools.partial(reduce_kernel, rank, states), in_specs=[...]
    all_gather x2 -> x0, blocking collectives: 31.7 us -> none  [body(): norms.append(lax.all_gather(norm_share, 'tensor', axis=0, tiled=True))]
    reduce_scatter x2 -> x0, waiting for transfers between devices: 21.2 us -> none  [body(): lax.psum_scatter(projected, 'tensor', scatter_dimension=0, tiled=True)]
    pallas_call x2 -> x1, Pallas kernels: 71.4 us -> 65.2 us  [scan_gate(): pl.pallas_call(functools.partial(scan_kernel, gated is not None), grid=(i...]
    reduce_sum x4 -> x0, other arithmetic: 4.07 us -> none  [the longest x2 2.04 us: normalize(): jnp.mean(dt_raw * dt_raw, axis=1, keepdims=True) + EPSILON]
    unnamed x51 -> x37, local copies, waits for them, and re-layouts: 17.9 us -> 13.9 us
    another operation x4 -> x0, other arithmetic: 3.82 us -> none
    pallas_call x2 -> x1, Pallas kernels: 14.5 us -> 12.1 us  [conv_project(): pl.pallas_call(conv_kernel, grid=(inner // BLOCK,), in_specs=[pl.BlockSpe...]
  transfers between devices with their start and end apart: 14 -> 12, of which waited for: 5 -> 3; matrix products, arithmetic and copies ran while one was open for 12% -> 10% of each run, Pallas kernels for 39% -> 69%
where the time goes in v2:
time: 163 us; the launch traced here: 160 us
  Pallas kernels  110 us (67%)
  local copies, waits for them, and re-layouts  25.1 us (15%)
  starting transfers between devices  15.7 us (10%)
  waiting for transfers between devices  4.76 us (3%)
  other arithmetic  3.78 us (2%)
    pallas_call x1, Pallas kernels, scan_gate(): pl.pallas_call(functools.partial(scan_kernel, gated is not None), grid=(i...  65.2 us
    pallas_call x1, Pallas kernels, reduce_norm(): pl.pallas_call(functools.partial(reduce_kernel, rank, states), in_specs=[...  32.6 us
    ppermute x12, starting transfers between devices, exchange(): lax.ppermute(block, 'dp', pairs[k])  15.7 us
    unnamed x37, local copies, waits for them, and re-layouts  13.9 us
    pallas_call x1, Pallas kernels, conv_project(): pl.pallas_call(conv_kernel, grid=(inner // BLOCK,), in_specs=[pl.BlockSpe...  12.1 us
    ppermute x12, waiting for transfers between devices, exchange(): lax.ppermute(block, 'dp', pairs[k])  4.76 us
  transfers between devices with their start and end apart: 12, of which 3 were waited for; matrix products, arithmetic and copies ran while one was open for 10% of the time, Pallas kernels for 69%

profile of v2, /device:TPU:0, one launch (start us, length us, event | category | flops | bytes accessed | tf_op | source)
XLA Modules:
  0.0 160.2 jit_solution(17694236831797041834)
XLA Ops:
  0.6 0.9 copy.87
  1.6 1.2 copy.86
  2.8 0.8 reshape.242
  3.6 0.2 convert_reduce_fusion
  3.8 0.1 broadcast_compare_fusion
  3.9 0.1 select_reduce_fusion
  4.1 0.1 copy.70
  4.2 0.1 reshape.299
  4.3 1.0 slice.63
  5.3 0.7 gather_fusion.7
  6.0 0.6 copy.79
  6.7 3.9 %collective-permute-start.11 = (bf16[2,3,2048]{2,0,1:T(2,128)(2,1)}, bf16[2,3,2048]{2,0,1:T(2,128)(2,1)S(1)}, u32[]{:S(2)}, u32[]{:S(2)}) collective-permute-start(bf16[2,3,2048]{2,0,1:T(2,128)(2,1)} %copy.79), channel_id=1, source_target_pairs={{0,24},{8,16},{16,8},{24,0},{1,25},{9,17},{17,9},{25,1},{2,26},{10... | collective-permute-start | bytes 73736 | tf_op jit(solution)/shard_map/ppermute | solution.py:435
  10.6 0.6 copy.77
  11.2 0.5 collective-permute-start.9
  11.8 0.1 broadcast_in_dim.21
  11.9 0.1 select_reduce_fusion.1
  12.0 0.1 copy.59
  12.1 0.6 gather_fusion
  12.7 0.1 reshape.243
  12.8 0.8 gather_fusion.1
  13.6 0.1 copy.75
  13.8 1.5 collective-permute-start.2
  15.3 1.5 collective-permute-start.1
  16.8 0.5 collective-permute-start
  17.4 0.1 fusion.1
  17.5 0.1 copy.66
  17.6 0.1 copy.68
  17.7 0.6 gather_fusion.5
  18.3 0.1 reshape.248
  18.4 0.1 copy.67
  18.5 0.1 reshape.275
  18.6 0.6 gather_fusion.3
  19.2 0.8 fusion.9
  20.1 0.6 copy.78
  20.7 3.1 %copy.65.xw_ref = bf16[2048,544]{1,0:T(8,128)(2,1)S(1)} copy(bf16[2048,544]{0,1:T(8,128)(2,1)} %param.17) | data formatting | bytes 4456448 | tf_op args[4]
  23.8 1.6 collective-permute-start.3
  25.3 0.1 collective-permute-start.5
  25.4 1.9 %collective-permute-start.4 = (bf16[2,16,2048]{2,1,0:T(8,128)(2,1)}, bf16[2,16,2048]{2,1,0:T(8,128)(2,1)}, u32[]{:S(2)}, u32[]{:S(2)}) collective-permute-start(bf16[2,16,2048]{2,1,0:T(8,128)(2,1)} %get-tuple-element.18), channel_id=1, source_target_pairs={{0,16},{8,24},{16,0},{24,8},{1,17},{9,25},{17,1},{25,9},{2,18},{10... | collective-permute-start | bytes 393224 | tf_op jit(solution)/shard_map/ppermute | solution.py:435
  27.3 0.9 pad_maximum_fusion.1
  28.3 0.7 gather_fusion.2
  29.0 0.1 copy.81
  29.1 2.2 %copy-done = bf16[8,128,2048]{2,1,0:T(8,128)(2,1)S(1)} copy-done((bf16[8,128,2048]{2,1,0:T(8,128)(2,1)S(1)}, bf16[8,128,2048]{2,1,0:T(8,128)(2,1)}, u32[]{:S(2)}) %copy-start) | copy-done | bytes 4194328
  31.3 12.1 %shard_map.148 = (bf16[1024,2048]{1,0:T(8,128)(2,1)S(1)}, f32[1024,544]{1,0:T(8,128)S(1)}) custom-call(bf16[8,128,2048]{2,1,0:T(8,128)(2,1)S(1)} %copy-done, f32[3,8,2048]{2,1,0:T(8,128)S(1)} %bitcast.40, f32[4,2048]{1,0:T(4,128)S(1)} %copy-done.3, f32[1,2048]{1,0:T(1,128)S(1)} %bitcast.41, bf16[2048,544]{1,0:T(8,128)(2,1)S(1)} %copy.65.xw_ref), custom_call_target="tpu_custom_call" | custom-call | flops 2281701376 | bytes 12845056 | tf_op jit(solution)/shard_map/pallas_call | solution.py:206
  43.4 1.9 %copy-done.7 = bf16[1024,2048]{1,0:T(8,128)(2,1)} copy-done((bf16[1024,2048]{1,0:T(8,128)(2,1)}, bf16[1024,2048]{1,0:T(8,128)(2,1)S(1)}, u32[]{:S(2)}) %copy-start.7) | copy-done | bytes 4194328
  45.4 32.6 %shard_map.149.norm_ref = bf16[1024,544]{1,0:T(8,128)(2,1)S(1)} custom-call(f32[1024,544]{1,0:T(8,128)S(1)} %get-tuple-element.7.proj_ref), custom_call_target="tpu_custom_call" | custom-call | flops 2228224 | bytes 40000000 | tf_op jit(solution)/shard_map/pallas_call | solution.py:137
  78.1 0.6 collective-permute-start.10
  78.6 1.1 pad_maximum_fusion
  79.7 0.6 gather_fusion.4
  80.4 0.0 copy-start.1
  80.4 1.6 copy-done.1
  82.0 65.2 %shard_map.150 = (bf16[8,128,2048]{2,1,0:T(8,128)(2,1)}, f32[8,16,2048]{2,1,0:T(8,128)S(1)}) custom-call(bf16[1024,544]{1,0:T(8,128)(2,1)S(1)} %shard_map.149.norm_ref, bf16[1024,2048]{1,0:T(8,128)(2,1)} %copy-done.7, bf16[8,128,2048]{2,1,0:T(8,128)(2,1)} %z_ref.1, bf16[512,2048]{1,0:T(8,128)(2,1)S(1)} %copy-done.1, f32[1,2048]{1,0:T(1,128)S(1)} %bitcast.42, ...), custom_call_target="tpu_custom_call" | custom-call | flops 2348810240 | bytes 14680064 | tf_op jit(solution)/shard_map/pallas_call | solution.py:367
  147.1 0.6 gather_fusion.6
  147.8 1.6 collective-permute-start.6
  149.3 1.5 collective-permute-start.8
  150.8 0.5 collective-permute-start.7
  151.4 0.9 maximum_convert_fusion.1
  152.2 1.3 scatter_fusion.1
  153.6 0.1 collective-permute-done.6
  153.7 3.2 %collective-permute-done.8 = bf16[2,16,2048]{2,1,0:T(8,128)(2,1)S(1)} collective-permute-done((bf16[2,16,2048]{2,1,0:T(8,128)(2,1)S(1)}, bf16[2,16,2048]{2,1,0:T(8,128)(2,1)S(1)}, u32[]{:S(2)}, u32[]{:S(2)}) %collective-permute-start.8) | collective-permute-done | bytes 131104 | tf_op jit(solution)/shard_map/ppermute | solution.py:435
  156.9 1.4 collective-permute-done.7
  158.3 0.1 maximum_convert_fusion
  158.4 0.9 scatter_fusion
  159.3 0.0 copy-start.11
  159.3 1.0 copy-done.11
  (54 shorter events, 0.4 us)
Async XLA Ops:
  0.6 11.1 %copy-start.14 = (s32[32]{0:T(128)S(1)}, s32[32]{0:T(128)}, u32[]{:S(2)}) copy-start(s32[32]{0:T(128)} %param.25) | copy-start | bytes 388
  2.8 17.2 %copy-start.9 = (f32[8,16,2048]{2,1,0:T(8,128)}, f32[8,16,2048]{2,1,0:T(8,128)S(1)}, u32[]{:S(2)}) copy-start(f32[8,16,2048]{2,1,0:T(8,128)S(1)} %copy.86) | copy-start | bytes 3145732
  6.7 144.2 %collective-permute-start.11 = (bf16[2,3,2048]{2,0,1:T(2,128)(2,1)}, bf16[2,3,2048]{2,0,1:T(2,128)(2,1)S(1)}, u32[]{:S(2)}, u32[]{:S(2)}) collective-permute-start(bf16[2,3,2048]{2,0,1:T(2,128)(2,1)} %copy.79), channel_id=1, source_target_pairs={{0,24},{8,16},{16,8},{24,0},{1,25},{9,17},{17,9},{25,1},{2,26},{10... | collective-permute-start | bytes 73736 | tf_op jit(solution)/shard_map/ppermute | solution.py:435
  11.2 140.1 %collective-permute-start.9 = (bf16[2,3,2048]{2,0,1:T(2,128)(2,1)}, bf16[2,3,2048]{2,0,1:T(2,128)(2,1)}, u32[]{:S(2)}, u32[]{:S(2)}) collective-permute-start(bf16[2,3,2048]{2,0,1:T(2,128)(2,1)} %copy.77), channel_id=1, source_target_pairs={{0,8},{8,0},{16,24},{24,16},{1,9},{9,1},{17,25},{25,17},{2,10},{10... | collective-permute-start | bytes 73736 | tf_op jit(solution)/shard_map/ppermute | solution.py:435
  13.8 10.0 %collective-permute-start.2 = (f32[3,2,2048]{2,0,1:T(4,128)S(1)}, f32[3,2,2048]{2,0,1:T(4,128)S(1)}, u32[]{:S(2)}, u32[]{:S(2)}) collective-permute-start(f32[3,2,2048]{2,0,1:T(4,128)S(1)} %get-tuple-element.20), channel_id=1, source_target_pairs={{0,24},{8,16},{16,8},{24,0},{1,25},{9,17},{17,9},{25,1},{2,26},{10... | collective-permute-start | bytes 147464 | tf_op jit(solution)/shard_map/ppermute | solution.py:435
  15.3 10.0 %collective-permute-start.1 = (f32[3,2,2048]{2,0,1:T(4,128)S(1)}, f32[3,2,2048]{2,0,1:T(4,128)S(1)}, u32[]{:S(2)}, u32[]{:S(2)}) collective-permute-start(f32[3,2,2048]{2,0,1:T(4,128)S(1)} %get-tuple-element.21), channel_id=1, source_target_pairs={{0,16},{8,24},{16,0},{24,8},{1,17},{9,25},{17,1},{25,9},{2,18},{10... | collective-permute-start | bytes 147464 | tf_op jit(solution)/shard_map/ppermute | solution.py:435
  16.8 8.6 %collective-permute-start = (f32[3,2,2048]{2,0,1:T(4,128)S(1)}, f32[3,2,2048]{2,0,1:T(4,128)}, u32[]{:S(2)}, u32[]{:S(2)}) collective-permute-start(f32[3,2,2048]{2,0,1:T(4,128)S(1)} %get-tuple-element.22), channel_id=1, source_target_pairs={{0,8},{8,0},{16,24},{24,16},{1,9},{9,1},{17,25},{25,17},{2,10},{10... | collective-permute-start | bytes 147464 | tf_op jit(solution)/shard_map/ppermute | solution.py:435
  20.7 8.4 %copy-start.3 = (f32[4,2048]{1,0:T(4,128)S(1)}, f32[4,2048]{1,0:T(4,128)}, u32[]{:S(2)}) copy-start(f32[4,2048]{1,0:T(4,128)} %cw_ref.1) | copy-start | bytes 98308
  20.7 8.4 %copy-start.4 = (f32[2048]{0:T(1024)S(1)}, f32[2048]{0:T(1024)}, u32[]{:S(2)}) copy-start(f32[2048]{0:T(1024)} %param.16) | copy-start | bytes 24580
  23.8 54.2 %collective-permute-start.3 = (bf16[2,16,2048]{2,1,0:T(8,128)(2,1)}, bf16[2,16,2048]{2,1,0:T(8,128)(2,1)}, u32[]{:S(2)}, u32[]{:S(2)}) collective-permute-start(bf16[2,16,2048]{2,1,0:T(8,128)(2,1)} %get-tuple-element.16), channel_id=1, source_target_pairs={{0,8},{8,0},{16,24},{24,16},{1,9},{9,1},{17,25},{25,17},{2,10},{10... | collective-permute-start | bytes 393224 | tf_op jit(solution)/shard_map/ppermute | solution.py:435
  25.3 53.3 %collective-permute-start.5 = (bf16[2,16,2048]{2,1,0:T(8,128)(2,1)}, bf16[2,16,2048]{2,1,0:T(8,128)(2,1)}, u32[]{:S(2)}, u32[]{:S(2)}) collective-permute-start(bf16[2,16,2048]{2,1,0:T(8,128)(2,1)} %get-tuple-element.17), channel_id=1, source_target_pairs={{0,24},{8,16},{16,8},{24,0},{1,25},{9,17},{17,9},{25,1},{2,26},{10... | collective-permute-start | bytes 393224 | tf_op jit(solution)/shard_map/ppermute | solution.py:435
  25.4 53.2 %collective-permute-start.4 = (bf16[2,16,2048]{2,1,0:T(8,128)(2,1)}, bf16[2,16,2048]{2,1,0:T(8,128)(2,1)}, u32[]{:S(2)}, u32[]{:S(2)}) collective-permute-start(bf16[2,16,2048]{2,1,0:T(8,128)(2,1)} %get-tuple-element.18), channel_id=1, source_target_pairs={{0,16},{8,24},{16,0},{24,8},{1,17},{9,25},{17,1},{25,9},{2,18},{10... | collective-permute-start | bytes 393224 | tf_op jit(solution)/shard_map/ppermute | solution.py:435
  29.1 2.2 %copy-start = (bf16[8,128,2048]{2,1,0:T(8,128)(2,1)S(1)}, bf16[8,128,2048]{2,1,0:T(8,128)(2,1)}, u32[]{:S(2)}) copy-start(bf16[8,128,2048]{2,1,0:T(8,128)(2,1)} %x_ref.1) | copy-start | bytes 12582916
  43.4 2.0 %copy-start.7 = (bf16[1024,2048]{1,0:T(8,128)(2,1)}, bf16[1024,2048]{1,0:T(8,128)(2,1)S(1)}, u32[]{:S(2)}) copy-start(bf16[1024,2048]{1,0:T(8,128)(2,1)S(1)} %get-tuple-element.8.x_ref) | copy-start | bytes 12582916
  45.4 32.7 %copy-start.13 = (bf16[2,3,2048]{2,0,1:T(2,128)(2,1)S(1)}, bf16[2,3,2048]{2,0,1:T(2,128)(2,1)}, u32[]{:S(2)}) copy-start(bf16[2,3,2048]{2,0,1:T(2,128)(2,1)} %copy.78) | copy-start | bytes 73732
  45.4 33.3 %copy-start.12 = (bf16[2,16,2048]{2,1,0:T(8,128)(2,1)S(1)}, bf16[2,16,2048]{2,1,0:T(8,128)(2,1)}, u32[]{:S(2)}) copy-start(bf16[2,16,2048]{2,1,0:T(8,128)(2,1)} %get-tuple-element.15) | copy-start | bytes 393220
  45.4 35.0 %copy-start.2 = (f32[16,2048]{1,0:T(8,128)S(1)}, f32[16,2048]{1,0:T(8,128)}, u32[]{:S(2)}) copy-start(f32[16,2048]{1,0:T(8,128)} %alog_ref.1) | copy-start | bytes 393220
  45.4 35.0 %copy-start.5 = (f32[2048]{0:T(1024)S(1)}, f32[2048]{0:T(1024)}, u32[]{:S(2)}) copy-start(f32[2048]{0:T(1024)} %param.19) | copy-start | bytes 24580
  45.4 35.0 %copy-start.6 = (f32[2048]{0:T(1024)S(1)}, f32[2048]{0:T(1024)}, u32[]{:S(2)}) copy-start(f32[2048]{0:T(1024)} %param.21) | copy-start | bytes 24580
  78.1 73.3 %collective-permute-start.10 = (bf16[2,3,2048]{2,0,1:T(2,128)(2,1)S(1)}, bf16[2,3,2048]{2,0,1:T(2,128)(2,1)S(1)}, u32[]{:S(2)}, u32[]{:S(2)}) collective-permute-start(bf16[2,3,2048]{2,0,1:T(2,128)(2,1)S(1)} %copy-done.13), channel_id=1, source_target_pairs={{0,16},{8,24},{16,0},{24,8},{1,17},{9,25},{17,1},{25,9},{2,18},{10... | collective-permute-start | bytes 73736 | tf_op jit(solution)/shard_map/ppermute | solution.py:435
  80.4 1.6 copy-start.1
  147.8 5.9 %collective-permute-start.6 = (bf16[2,16,2048]{2,1,0:T(8,128)(2,1)S(1)}, bf16[2,16,2048]{2,1,0:T(8,128)(2,1)S(1)}, u32[]{:S(2)}, u32[]{:S(2)}) collective-permute-start(bf16[2,16,2048]{2,1,0:T(8,128)(2,1)S(1)} %get-tuple-element.12), channel_id=1, source_target_pairs={{0,8},{8,0},{16,24},{24,16},{1,9},{9,1},{17,25},{25,17},{2,10},{10... | collective-permute-start | bytes 393224 | tf_op jit(solution)/shard_map/ppermute | solution.py:435
  149.3 7.6 %collective-permute-start.8 = (bf16[2,16,2048]{2,1,0:T(8,128)(2,1)S(1)}, bf16[2,16,2048]{2,1,0:T(8,128)(2,1)S(1)}, u32[]{:S(2)}, u32[]{:S(2)}) collective-permute-start(bf16[2,16,2048]{2,1,0:T(8,128)(2,1)S(1)} %get-tuple-element.13), channel_id=1, source_target_pairs={{0,24},{8,16},{16,8},{24,0},{1,25},{9,17},{17,9},{25,1},{2,26},{10... | collective-permute-start | bytes 393224 | tf_op jit(solution)/shard_map/ppermute | solution.py:435
  150.8 7.5 %collective-permute-start.7 = (bf16[2,16,2048]{2,1,0:T(8,128)(2,1)S(1)}, bf16[2,16,2048]{2,1,0:T(8,128)(2,1)S(1)}, u32[]{:S(2)}, u32[]{:S(2)}) collective-permute-start(bf16[2,16,2048]{2,1,0:T(8,128)(2,1)S(1)} %get-tuple-element.14), channel_id=1, source_target_pairs={{0,16},{8,24},{16,0},{24,8},{1,17},{9,25},{17,1},{25,9},{2,18},{10... | collective-permute-start | bytes 393224 | tf_op jit(solution)/shard_map/ppermute | solution.py:435
  152.2 6.2 %copy-start.10 = (f32[8,16,2048]{2,1,0:T(8,128)S(1)}, f32[8,16,2048]{2,1,0:T(8,128)}, u32[]{:S(2)}) copy-start(f32[8,16,2048]{2,1,0:T(8,128)} %copy-done.9) | copy-start | bytes 3145732
  153.6 5.7 %copy-start.8 = (f32[8,3,2048]{2,0,1:T(8,128)}, f32[8,3,2048]{2,0,1:T(8,128)S(1)}, u32[]{:S(2)}) copy-start(f32[8,3,2048]{2,0,1:T(8,128)S(1)} %scatter_fusion.1) | copy-start | bytes 589828
  159.3 1.0 copy-start.11

commit v3 on v2

--- a/solution.py
+++ b/solution.py
@@ -9,7 +9,6 @@
 
 EPSILON = 1e-06
 NORM_FLOOR = 0.25
-LOG2E = 1.4426950408889634
 CHUNKS = 1
 BLOCK = 256
 LANES = 128
@@ -287,7 +286,7 @@
 
     for part in range(width // LANES):
         lanes = slice(part * LANES, (part + 1) * LANES)
-        rates = -jnp.exp(alog_ref[:, lanes]) * LOG2E
+        rates = -jnp.exp(alog_ref[:, lanes])
         rates = [jnp.broadcast_to(rates[n : n + 1], (requests, LANES)) for n in range(states)]
         start = jnp.swapaxes(state_ref[:, :, lanes].astype(jnp.float32), 0, 1)
         unroll = 8
@@ -301,7 +300,7 @@
                 drive = drive_s[row, lanes]
                 sums = [y_s[row, lanes], None, None, None]
                 for n in range(states):
-                    held[n] = jnp.exp2(dt * rates[n]) * held[n] + drive * bc_s[t, n]
+                    held[n] = jnp.exp(dt * rates[n]) * held[n] + drive * bc_s[t, n]
                     term = held[n] * bc_s[t, states + n]
                     q = n % 4
                     sums[q] = term if sums[q] is None else sums[q] + term
@@ -455,26 +454,8 @@
     conv_got = exchange([conv_rows[:, k] for k in range(groups)])
     conv_start = jnp.concatenate(conv_got, axis=1)[:, lookup]
 
-    ssm_rows = ssm_cache[wanted].astype(jnp.bfloat16)
-    ssm_got = exchange([ssm_rows[k] for k in range(groups)])
-    state = jnp.concatenate(ssm_got, axis=0)[lookup]
-
-    own_placed = (own_holders[None, None, :] == sent_to[:, None, None]) & (
-        own_ranks[None, None, :] == rank_range[None, :, None]
-    )
-    picked_rows = jnp.sum(
-        jnp.where(own_placed, jnp.arange(requests, dtype=jnp.int32)[None, None, :], 0), axis=2
-    )
-    targets = jnp.where(occupied, sources, slot_count)[came_from].reshape(-1)
-
-    last_inputs = hidden_x[:, whole - kept_rows :, :][picked_rows]
-    last_got = exchange([last_inputs[k] for k in range(groups)])
-    new_conv = conv_cache.at[targets].set(
-        jnp.concatenate(last_got, axis=0).astype(jnp.float32), mode="drop"
-    )
-
     turn = whole // CHUNKS
-    conv_outs, norms = [], []
+    conv_outs, products = [], []
     for chunk in range(CHUNKS):
         if chunk == 0:
             start = conv_start
@@ -486,7 +467,30 @@
             chunk, turn, hidden_x, start, conv_weight, conv_bias, x_weight
         )
         conv_outs.append(conv_out)
-        norms.append(reduce_norm(projected, rank_width, state_width))
+        products.append(projected)
+
+    wanted_late, targets_late, products[0] = lax.optimization_barrier(
+        (wanted, sent_to, products[0])
+    )
+    ssm_rows = ssm_cache[wanted_late].astype(jnp.bfloat16)
+    ssm_got = exchange([ssm_rows[k] for k in range(groups)])
+    state = jnp.concatenate(ssm_got, axis=0)[lookup]
+
+    own_placed = (own_holders[None, None, :] == targets_late[:, None, None]) & (
+        own_ranks[None, None, :] == rank_range[None, :, None]
+    )
+    picked_rows = jnp.sum(
+        jnp.where(own_placed, jnp.arange(requests, dtype=jnp.int32)[None, None, :], 0), axis=2
+    )
+    targets = jnp.where(occupied, sources, slot_count)[came_from].reshape(-1)
+
+    last_inputs = hidden_x[:, whole - kept_rows :, :][picked_rows]
+    last_got = exchange([last_inputs[k] for k in range(groups)])
+    new_conv = conv_cache.at[targets].set(
+        jnp.concatenate(last_got, axis=0).astype(jnp.float32), mode="drop"
+    )
+
+    norms = [reduce_norm(product, rank_width, state_width) for product in products]
 
     gated = None
     for chunk in range(CHUNKS):

time: 163 us -> 173 us (1.061)
  local copies, waits for them, and re-layouts: 25.1 us -> 30.7 us
  Pallas kernels: 110 us -> 114 us
    pallas_call x1, Pallas kernels: 65.2 us -> 69.2 us  [scan_gate(): pl.pallas_call(functools.partial(scan_kernel, gated is not None), grid=(i...]
    unnamed x37 -> x41, local copies, waits for them, and re-layouts: 13.9 us -> 17.6 us
  transfers between devices with their start and end apart: 12 -> 12, of which waited for: 3 -> 3; matrix products, arithmetic and copies ran while one was open for 10% -> 6% of each run, Pallas kernels for 69% -> 60%
where the time goes in v3:
time: 173 us; the launch traced here: 170 us
  Pallas kernels  114 us (66%)
  local copies, waits for them, and re-layouts  30.7 us (18%)
  starting transfers between devices  15.6 us (9%)
  waiting for transfers between devices  5.5 us (3%)
  other arithmetic  2.94 us (2%)
    pallas_call x1, Pallas kernels, scan_gate(): pl.pallas_call(functools.partial(scan_kernel, gated is not None), grid=(i...  69.2 us
    pallas_call x1, Pallas kernels, reduce_norm(): pl.pallas_call(functools.partial(reduce_kernel, rank, states), in_specs=[...  32.6 us
    unnamed x41, local copies, waits for them, and re-layouts  17.6 us
    ppermute x12, starting transfers between devices, exchange(): lax.ppermute(block, 'dp', pairs[k])  15.6 us
    pallas_call x1, Pallas kernels, conv_project(): pl.pallas_call(conv_kernel, grid=(inner // BLOCK,), in_specs=[pl.BlockSpe...  12.1 us
    ppermute x12, waiting for transfers between devices, exchange(): lax.ppermute(block, 'dp', pairs[k])  5.5 us
  transfers between devices with their start and end apart: 12, of which 3 were waited for; matrix products, arithmetic and copies ran while one was open for 6% of the time, Pallas kernels for 60%

profile of v3, /device:TPU:0, one launch (start us, length us, event | category | flops | bytes accessed | tf_op | source)
XLA Modules:
  0.0 169.7 jit_solution(1381463087640985326)
XLA Ops:
  0.6 0.9 copy.77
  1.6 2.3 %copy.76 = f32[8,16,2048]{2,1,0:T(8,128)} copy(f32[8,16,2048]{2,1,0:T(8,128)} %param.22) | data formatting | bytes 2097152
  3.9 0.7 reshape.224
  4.6 0.2 convert_reduce_fusion
  4.8 0.7 broadcast_in_dim.23
  5.6 0.1 select_reduce_fusion.1
  5.7 0.1 copy.51
  5.8 0.6 gather_fusion
  6.4 0.1 reshape.225
  6.5 0.8 gather_fusion.1
  7.3 0.1 copy.65
  7.5 4.0 %collective-permute-start.2 = (f32[3,2,2048]{2,0,1:T(4,128)S(1)}, f32[3,2,2048]{2,0,1:T(4,128)S(1)}, u32[]{:S(2)}, u32[]{:S(2)}) collective-permute-start(f32[3,2,2048]{2,0,1:T(4,128)S(1)} %get-tuple-element.26), channel_id=1, source_target_pairs={{0,24},{8,16},{16,8},{24,0},{1,25},{9,17},{17,9},{25,1},{2,26},{10... | collective-permute-start | bytes 147464 | tf_op jit(solution)/shard_map/ppermute | solution.py:434
  11.5 0.5 collective-permute-start.1
  12.0 0.1 collective-permute-start
  12.2 0.1 fusion.1
  12.3 0.1 copy.58
  12.5 0.6 gather_fusion.5
  13.0 0.1 reshape.230
  13.1 1.0 slice.63
  14.2 0.0 copy-start.8
  14.2 3.1 %copy.57.xw_ref = bf16[2048,544]{1,0:T(8,128)(2,1)S(1)} copy(bf16[2048,544]{0,1:T(8,128)(2,1)} %param.17) | data formatting | bytes 4456448 | tf_op args[4]
  17.3 0.6 copy-done.16
  17.9 0.9 pad_maximum_fusion.1
  18.9 0.7 gather_fusion.2
  19.6 0.1 copy.71
  19.7 0.0 copy-start.4
  19.7 2.2 %copy-done.4 = bf16[8,128,2048]{2,1,0:T(8,128)(2,1)S(1)} copy-done((bf16[8,128,2048]{2,1,0:T(8,128)(2,1)S(1)}, bf16[8,128,2048]{2,1,0:T(8,128)(2,1)}, u32[]{:S(2)}) %copy-start.4) | copy-done | bytes 4194328
  21.9 12.1 %shard_map.148 = (bf16[1024,2048]{1,0:T(8,128)(2,1)S(1)}, f32[1024,544]{1,0:T(8,128)S(1)}) custom-call(bf16[8,128,2048]{2,1,0:T(8,128)(2,1)S(1)} %copy-done.4, f32[3,8,2048]{2,1,0:T(8,128)S(1)} %bitcast.36, f32[4,2048]{1,0:T(4,128)S(1)} %copy-done.7, f32[1,2048]{1,0:T(1,128)S(1)} %bitcast.37, bf16[2048,544]{1,0:T(8,128)(2,1)S(1)} %copy.57.xw_ref), custom_call_target="tpu_custom_call" | custom-call | flops 2281701376 | bytes 12845056 | tf_op jit(solution)/shard_map/pallas_call | solution.py:205
  34.0 0.0 copy-start
  34.0 1.5 copy-done
  35.5 1.9 %copy-done.11 = bf16[1024,2048]{1,0:T(8,128)(2,1)} copy-done((bf16[1024,2048]{1,0:T(8,128)(2,1)}, bf16[1024,2048]{1,0:T(8,128)(2,1)S(1)}, u32[]{:S(2)}) %copy-start.11) | copy-done | bytes 4194328
  37.5 0.1 broadcast_compare_fusion
  37.5 0.1 select_reduce_fusion
  37.7 0.1 copy.60
  37.8 0.1 reshape.281
  37.9 0.1 reshape.257
  38.0 2.1 %gather_fusion.3 = bf16[8,16,2048]{2,1,0:T(8,128)(2,1)S(1)} fusion(f32[8,16,2048]{2,1,0:T(8,128)} %copy.76, s32[1024]{0:T(1024)S(1)} %pad_clamp_fusion.1), kind=kCustom, calls=%fused_computation.3 | custom fusion | bytes 1048608 | tf_op jit(solution)/shard_map/gather | solution.py:475
  40.1 0.8 fusion.9
  40.8 1.9 %collective-permute-start.3 = (bf16[2,16,2048]{2,1,0:T(8,128)(2,1)}, bf16[2,16,2048]{2,1,0:T(8,128)(2,1)S(1)}, u32[]{:S(2)}, u32[]{:S(2)}) collective-permute-start(bf16[2,16,2048]{2,1,0:T(8,128)(2,1)} %get-tuple-element.22), channel_id=1, source_target_pairs={{0,8},{8,0},{16,24},{24,16},{1,9},{9,1},{17,25},{25,17},{2,10},{10... | collective-permute-start | bytes 393224 | tf_op jit(solution)/shard_map/ppermute | solution.py:434
  42.7 1.5 collective-permute-start.5
  44.2 0.1 collective-permute-start.4
  44.3 0.7 gather_fusion.7
  45.2 2.9 %collective-permute-start.11 = (bf16[2,3,2048]{2,0,1:T(2,128)(2,1)S(1)}, bf16[2,3,2048]{2,0,1:T(2,128)(2,1)S(1)}, u32[]{:S(2)}, u32[]{:S(2)}) collective-permute-start(bf16[2,3,2048]{2,0,1:T(2,128)(2,1)S(1)} %copy.69), channel_id=1, source_target_pairs={{0,24},{8,16},{16,8},{24,0},{1,25},{9,17},{17,9},{25,1},{2,26},{10... | collective-permute-start | bytes 73736 | tf_op jit(solution)/shard_map/ppermute | solution.py:434
  48.2 0.5 collective-permute-start.9
  48.7 32.6 %shard_map.149.norm_ref = bf16[1024,544]{1,0:T(8,128)(2,1)S(1)} custom-call(f32[1024,544]{1,0:T(8,128)S(1)} %copy-done.1), custom_call_target="tpu_custom_call" | custom-call | flops 2228224 | bytes 40000000 | tf_op jit(solution)/shard_map/pallas_call | solution.py:136
  81.3 1.0 copy-done.2
  82.4 0.5 collective-permute-start.10
  82.9 1.0 pad_maximum_fusion
  83.8 0.6 gather_fusion.4
  84.5 1.3 copy-done.3
  85.8 1.6 copy-done.5
  87.4 69.2 %shard_map.150 = (bf16[8,128,2048]{2,1,0:T(8,128)(2,1)}, f32[8,16,2048]{2,1,0:T(8,128)S(1)}) custom-call(bf16[1024,544]{1,0:T(8,128)(2,1)S(1)} %copy-done.3, bf16[1024,2048]{1,0:T(8,128)(2,1)} %copy-done.11, bf16[8,128,2048]{2,1,0:T(8,128)(2,1)} %z_ref.1, bf16[512,2048]{1,0:T(8,128)(2,1)S(1)} %copy-done.5, f32[1,2048]{1,0:T(1,128)S(1)} %bitcast.38, ...), custom_call_target="tpu_custom_call" | custom-call | flops 2348810240 | bytes 14680064 | tf_op jit(solution)/shard_map/pallas_call | solution.py:366
  156.6 0.6 gather_fusion.6
  157.2 1.6 collective-permute-start.6
  158.8 1.5 collective-permute-start.8
  160.3 0.5 collective-permute-start.7
  160.8 0.1 maximum_convert_fusion.1
  160.9 1.3 scatter_fusion.1
  162.3 0.9 collective-permute-done.6
  163.1 3.2 %collective-permute-done.8 = bf16[2,16,2048]{2,1,0:T(8,128)(2,1)S(1)} collective-permute-done((bf16[2,16,2048]{2,1,0:T(8,128)(2,1)S(1)}, bf16[2,16,2048]{2,1,0:T(8,128)(2,1)S(1)}, u32[]{:S(2)}, u32[]{:S(2)}) %collective-permute-start.8) | collective-permute-done | bytes 131104 | tf_op jit(solution)/shard_map/ppermute | solution.py:434
  166.4 1.4 collective-permute-done.7
  167.7 0.1 maximum_convert_fusion
  167.8 0.9 scatter_fusion
  168.7 1.0 copy-done.14
  (56 shorter events, 0.5 us)
Async XLA Ops:
  7.5 9.7 %collective-permute-start.2 = (f32[3,2,2048]{2,0,1:T(4,128)S(1)}, f32[3,2,2048]{2,0,1:T(4,128)S(1)}, u32[]{:S(2)}, u32[]{:S(2)}) collective-permute-start(f32[3,2,2048]{2,0,1:T(4,128)S(1)} %get-tuple-element.26), channel_id=1, source_target_pairs={{0,24},{8,16},{16,8},{24,0},{1,25},{9,17},{17,9},{25,1},{2,26},{10... | collective-permute-start | bytes 147464 | tf_op jit(solution)/shard_map/ppermute | solution.py:434
  11.5 5.7 %collective-permute-start.1 = (f32[3,2,2048]{2,0,1:T(4,128)S(1)}, f32[3,2,2048]{2,0,1:T(4,128)}, u32[]{:S(2)}, u32[]{:S(2)}) collective-permute-start(f32[3,2,2048]{2,0,1:T(4,128)S(1)} %get-tuple-element.27), channel_id=1, source_target_pairs={{0,16},{8,24},{16,0},{24,8},{1,17},{9,25},{17,1},{25,9},{2,18},{10... | collective-permute-start | bytes 147464 | tf_op jit(solution)/shard_map/ppermute | solution.py:434
  12.0 5.3 %collective-permute-start = (f32[3,2,2048]{2,0,1:T(4,128)S(1)}, f32[3,2,2048]{2,0,1:T(4,128)S(1)}, u32[]{:S(2)}, u32[]{:S(2)}) collective-permute-start(f32[3,2,2048]{2,0,1:T(4,128)S(1)} %get-tuple-element.28), channel_id=1, source_target_pairs={{0,8},{8,0},{16,24},{24,16},{1,9},{9,1},{17,25},{25,17},{2,10},{10... | collective-permute-start | bytes 147464 | tf_op jit(solution)/shard_map/ppermute | solution.py:434
  14.1 5.5 %copy-start.7 = (f32[4,2048]{1,0:T(4,128)S(1)}, f32[4,2048]{1,0:T(4,128)}, u32[]{:S(2)}) copy-start(f32[4,2048]{1,0:T(4,128)} %cw_ref.1) | copy-start | bytes 98308
  14.2 5.5 %copy-start.8 = (f32[2048]{0:T(1024)S(1)}, f32[2048]{0:T(1024)}, u32[]{:S(2)}) copy-start(f32[2048]{0:T(1024)} %param.16) | copy-start | bytes 24580
  17.3 0.6 copy-start.16
  19.7 2.2 %copy-start.4 = (bf16[8,128,2048]{2,1,0:T(8,128)(2,1)S(1)}, bf16[8,128,2048]{2,1,0:T(8,128)(2,1)}, u32[]{:S(2)}) copy-start(bf16[8,128,2048]{2,1,0:T(8,128)(2,1)} %x_ref.1) | copy-start | bytes 12582916
  34.0 1.5 copy-start
  35.5 1.9 %copy-start.11 = (bf16[1024,2048]{1,0:T(8,128)(2,1)}, bf16[1024,2048]{1,0:T(8,128)(2,1)S(1)}, u32[]{:S(2)}) copy-start(bf16[1024,2048]{1,0:T(8,128)(2,1)S(1)} %get-tuple-element.12.x_ref) | copy-start | bytes 12582916
  37.4 11.2 %copy-start.1 = (f32[1024,544]{1,0:T(8,128)S(1)}, f32[1024,544]{1,0:T(8,128)}, u32[]{:S(2)}) copy-start(f32[1024,544]{1,0:T(8,128)} %copy-done) | copy-start | bytes 6684676
  40.8 42.0 %copy-start.15 = (bf16[2,16,2048]{2,1,0:T(8,128)(2,1)S(1)}, bf16[2,16,2048]{2,1,0:T(8,128)(2,1)}, u32[]{:S(2)}) copy-start(bf16[2,16,2048]{2,1,0:T(8,128)(2,1)} %get-tuple-element.21) | copy-start | bytes 393220
  40.8 41.5 %collective-permute-start.3 = (bf16[2,16,2048]{2,1,0:T(8,128)(2,1)}, bf16[2,16,2048]{2,1,0:T(8,128)(2,1)S(1)}, u32[]{:S(2)}, u32[]{:S(2)}) collective-permute-start(bf16[2,16,2048]{2,1,0:T(8,128)(2,1)} %get-tuple-element.22), channel_id=1, source_target_pairs={{0,8},{8,0},{16,24},{24,16},{1,9},{9,1},{17,25},{25,17},{2,10},{10... | collective-permute-start | bytes 393224 | tf_op jit(solution)/shard_map/ppermute | solution.py:434
  42.7 40.1 %collective-permute-start.5 = (bf16[2,16,2048]{2,1,0:T(8,128)(2,1)}, bf16[2,16,2048]{2,1,0:T(8,128)(2,1)S(1)}, u32[]{:S(2)}, u32[]{:S(2)}) collective-permute-start(bf16[2,16,2048]{2,1,0:T(8,128)(2,1)} %get-tuple-element.23), channel_id=1, source_target_pairs={{0,24},{8,16},{16,8},{24,0},{1,25},{9,17},{17,9},{25,1},{2,26},{10... | collective-permute-start | bytes 393224 | tf_op jit(solution)/shard_map/ppermute | solution.py:434
  44.2 38.6 %collective-permute-start.4 = (bf16[2,16,2048]{2,1,0:T(8,128)(2,1)}, bf16[2,16,2048]{2,1,0:T(8,128)(2,1)}, u32[]{:S(2)}, u32[]{:S(2)}) collective-permute-start(bf16[2,16,2048]{2,1,0:T(8,128)(2,1)} %get-tuple-element.24), channel_id=1, source_target_pairs={{0,16},{8,24},{16,0},{24,8},{1,17},{9,25},{17,1},{25,9},{2,18},{10... | collective-permute-start | bytes 393224 | tf_op jit(solution)/shard_map/ppermute | solution.py:434
  45.2 39.2 %copy-start.6 = (f32[16,2048]{1,0:T(8,128)S(1)}, f32[16,2048]{1,0:T(8,128)}, u32[]{:S(2)}) copy-start(f32[16,2048]{1,0:T(8,128)} %alog_ref.1) | copy-start | bytes 393220
  45.2 39.2 %copy-start.9 = (f32[2048]{0:T(1024)S(1)}, f32[2048]{0:T(1024)}, u32[]{:S(2)}) copy-start(f32[2048]{0:T(1024)} %param.19) | copy-start | bytes 24580
  45.2 39.2 %copy-start.10 = (f32[2048]{0:T(1024)S(1)}, f32[2048]{0:T(1024)}, u32[]{:S(2)}) copy-start(f32[2048]{0:T(1024)} %param.21) | copy-start | bytes 24580
  45.2 115.0 %collective-permute-start.11 = (bf16[2,3,2048]{2,0,1:T(2,128)(2,1)S(1)}, bf16[2,3,2048]{2,0,1:T(2,128)(2,1)S(1)}, u32[]{:S(2)}, u32[]{:S(2)}) collective-permute-start(bf16[2,3,2048]{2,0,1:T(2,128)(2,1)S(1)} %copy.69), channel_id=1, source_target_pairs={{0,24},{8,16},{16,8},{24,0},{1,25},{9,17},{17,9},{25,1},{2,26},{10... | collective-permute-start | bytes 73736 | tf_op jit(solution)/shard_map/ppermute | solution.py:434
  48.2 112.6 %collective-permute-start.9 = (bf16[2,3,2048]{2,0,1:T(2,128)(2,1)S(1)}, bf16[2,3,2048]{2,0,1:T(2,128)(2,1)S(1)}, u32[]{:S(2)}, u32[]{:S(2)}) collective-permute-start(bf16[2,3,2048]{2,0,1:T(2,128)(2,1)S(1)} %copy.67), channel_id=1, source_target_pairs={{0,8},{8,0},{16,24},{24,16},{1,9},{9,1},{17,25},{25,17},{2,10},{10... | collective-permute-start | bytes 73736 | tf_op jit(solution)/shard_map/ppermute | solution.py:434
  81.3 1.1 copy-start.2
  82.4 78.4 %collective-permute-start.10 = (bf16[2,3,2048]{2,0,1:T(2,128)(2,1)S(1)}, bf16[2,3,2048]{2,0,1:T(2,128)(2,1)S(1)}, u32[]{:S(2)}, u32[]{:S(2)}) collective-permute-start(bf16[2,3,2048]{2,0,1:T(2,128)(2,1)S(1)} %copy.68), channel_id=1, source_target_pairs={{0,16},{8,24},{16,0},{24,8},{1,17},{9,25},{17,1},{25,9},{2,18},{10... | collective-permute-start | bytes 73736 | tf_op jit(solution)/shard_map/ppermute | solution.py:434
  84.5 1.3 copy-start.3
  85.8 1.6 copy-start.5
  157.2 5.9 %collective-permute-start.6 = (bf16[2,16,2048]{2,1,0:T(8,128)(2,1)S(1)}, bf16[2,16,2048]{2,1,0:T(8,128)(2,1)S(1)}, u32[]{:S(2)}, u32[]{:S(2)}) collective-permute-start(bf16[2,16,2048]{2,1,0:T(8,128)(2,1)S(1)} %get-tuple-element.18), channel_id=1, source_target_pairs={{0,8},{8,0},{16,24},{24,16},{1,9},{9,1},{17,25},{25,17},{2,10},{10... | collective-permute-start | bytes 393224 | tf_op jit(solution)/shard_map/ppermute | solution.py:434
  158.8 7.6 %collective-permute-start.8 = (bf16[2,16,2048]{2,1,0:T(8,128)(2,1)S(1)}, bf16[2,16,2048]{2,1,0:T(8,128)(2,1)S(1)}, u32[]{:S(2)}, u32[]{:S(2)}) collective-permute-start(bf16[2,16,2048]{2,1,0:T(8,128)(2,1)S(1)} %get-tuple-element.19), channel_id=1, source_target_pairs={{0,24},{8,16},{16,8},{24,0},{1,25},{9,17},{17,9},{25,1},{2,26},{10... | collective-permute-start | bytes 393224 | tf_op jit(solution)/shard_map/ppermute | solution.py:434
  160.3 7.5 %collective-permute-start.7 = (bf16[2,16,2048]{2,1,0:T(8,128)(2,1)S(1)}, bf16[2,16,2048]{2,1,0:T(8,128)(2,1)S(1)}, u32[]{:S(2)}, u32[]{:S(2)}) collective-permute-start(bf16[2,16,2048]{2,1,0:T(8,128)(2,1)S(1)} %get-tuple-element.20), channel_id=1, source_target_pairs={{0,16},{8,24},{16,0},{24,8},{1,17},{9,25},{17,1},{25,9},{2,18},{10... | collective-permute-start | bytes 393224 | tf_op jit(solution)/shard_map/ppermute | solution.py:434
  160.9 6.9 %copy-start.13 = (f32[8,16,2048]{2,1,0:T(8,128)S(1)}, f32[8,16,2048]{2,1,0:T(8,128)}, u32[]{:S(2)}) copy-start(f32[8,16,2048]{2,1,0:T(8,128)} %copy.76) | copy-start | bytes 3145732
  162.2 6.5 %copy-start.12 = (f32[8,3,2048]{2,0,1:T(8,128)}, f32[8,3,2048]{2,0,1:T(8,128)S(1)}, u32[]{:S(2)}) copy-start(f32[8,3,2048]{2,0,1:T(8,128)S(1)} %scatter_fusion.1) | copy-start | bytes 589828
  168.7 1.0 copy-start.14
